TPU v7x, 256 devices: a whole 4x4x8 slice. The times are simulated.
256 devices in a mesh: kx: 8 (over z), ht: 8 (over y, core), real: 4 (over x).
Axes of the slice: x: 4, y: 4, z: 8, core: 2. Of those that a mesh axis runs over, the one named last changes fastest.
Arguments:
- velocity: float32 [3, 4, 32, 512, 128], P(None, 'real', 'kx', 'ht'), may hold values from -6 to 6
- low_index: int32 [8], replicated, may hold values from 0 to 31, as said below
- neighbours: int32 [32, 8], P('kx'), may hold values from 0 to 31, as said below
- owner_map: int32 [64], replicated, may hold values from 0 to 63, each once
- mode_counts: int32 [32], P('kx'), may hold values from 16 to 64
- helmholtz: float32 [64, 512, 512], P(('kx', 'ht')), may hold values from -0.25 to 0.25
Outputs:
- velocity_next: float32 [3, 4, 32, 512, 128], P(None, 'real', 'kx', 'ht')
Inputs may be any that keep to these rules, and one draw needn't show every extreme that they name: `low_index`: distinct values. neighbours[m, j] lies within 4 modes of m, counting circularly over the 32 modes; offsets of + 4 and - 4 both occur.
All inputs are finite; a program needn't handle non-finite values.
Results may differ from a plain program's by a relative error of at most 0.0001.
Values sent between devices are 32-bit elements; how exact they have to be, the bound alone decides.
A program may use at most 64 MiB of HBM per device.

v0:
```python
import jax
import jax.numpy as jnp
from jax import lax
from jax.sharding import PartitionSpec as P

dt_step = 0.1


def extended_2(block, sides, width):
    for axis, dim in sides:
        count = lax.axis_size(axis)
        forward = [(i, i + 1) for i in range(count - 1)]
        forward.append((count - 1, 0))
        backward = [(target, source) for source, target in forward]
        low = lax.ppermute(
            lax.slice_in_dim(block, block.shape[dim] - width, None, axis=dim), axis, forward
        )
        high = lax.ppermute(lax.slice_in_dim(block, 0, width, axis=dim), axis, backward)
        block = jnp.concatenate([low, block, high], axis=dim)
    return block


def spanwise_tables(mode_count, point_count):
    column_ids = jnp.arange(2 * mode_count)
    wavenumber = (column_ids // 2).astype(jnp.float32)
    imag_part = column_ids % 2
    positions = 2.0 * jnp.pi * jnp.arange(point_count).astype(jnp.float32) / point_count
    phases = wavenumber[:, None] * positions[None, :]
    forward = jnp.where(imag_part[:, None] == 0, jnp.cos(phases), -jnp.sin(phases)) / jnp.sqrt(
        jnp.float32(mode_count)
    )
    backward = forward.T * (2.0 * mode_count / point_count)
    return (forward, backward)


def apply_inverse(block, helmholtz, kx_count, ht_count, slots_dev, rows_ht):
    components, reals_dev, band_modes = (block.shape[0], block.shape[1], block.shape[2])
    regrouped = block.reshape(
        components, reals_dev, band_modes, kx_count, ht_count, slots_dev, 2, rows_ht
    )
    regrouped = regrouped.transpose(0, 1, 3, 2, 5, 6, 4, 7)
    regrouped = regrouped.reshape(
        components, reals_dev, kx_count * band_modes, slots_dev, 2, ht_count * rows_ht
    )
    solved = jnp.einsum("syx,crmspx->crmspy", helmholtz, regrouped, precision=lax.Precision.HIGHEST)
    solved = solved.reshape(
        components, reals_dev, kx_count, band_modes, slots_dev, 2, ht_count, rows_ht
    )
    solved = solved.transpose(0, 1, 3, 2, 6, 4, 5, 7)
    return solved.reshape(block.shape)


def local(velocity, low_index, neighbours, owner_map, mode_counts, helmholtz):
    highest = lax.Precision.HIGHEST
    components, reals_dev, band_modes, rows_ht, columns = velocity.shape
    kz_modes = columns // 2
    forward, backward = spanwise_tables(kz_modes, 4 * kz_modes)
    kx_count = lax.axis_size("kx")
    ht_count = lax.axis_size("ht")
    kx_total = band_modes * kx_count
    realizations = reals_dev * lax.axis_size("real")
    owners = kx_count * ht_count
    slots_dev = kz_modes // owners
    width_out = slots_dev * 2 * rows_ht
    low_members = low_index.shape[0]
    band_start = lax.axis_index("kx") * band_modes
    global_modes = band_start + jnp.arange(band_modes, dtype=jnp.int32)
    low_select = (low_index[:, None] == global_modes[None, :]).astype(jnp.float32)
    high_mask = 1.0 - jnp.sum(low_select, axis=0)
    offsets = (neighbours - global_modes[:, None] + kx_total // 2) % kx_total - kx_total // 2
    local_partner = jnp.arange(band_modes, dtype=jnp.int32)[:, None] + band_modes + offsets
    column_mask = ((jnp.arange(columns) // 2)[None, :] < mode_counts[:, None]).astype(jnp.float32)
    inverse_map = (
        jnp.zeros((kz_modes,), jnp.int32).at[owner_map].set(jnp.arange(kz_modes, dtype=jnp.int32))
    )
    current = velocity
    physical = jnp.dot(current, forward, precision=highest)
    extended = extended_2(physical, (("kx", 2),), band_modes)
    own_low = jnp.einsum("jm,crmyz->crjyz", low_select, physical, precision=highest)
    low_fields = lax.psum(own_low, "kx")
    high_low = jnp.zeros_like(physical)
    stresses = []
    for member in range(low_members):
        partner = jnp.take(extended, local_partner[:, member], axis=2)
        low_one = low_fields[:, :, member : member + 1]
        high_low = high_low + low_one * partner[1:2] + partner * low_one[1:2]
        weighted = physical * (partner[1:2] * high_mask[None, None, :, None, None])
        stresses.append(jnp.sum(weighted, axis=(1, 2)))
    stress = jnp.stack(stresses, axis=1)
    nonlinear = jnp.dot(high_low, backward, precision=highest)
    summed = lax.psum(stress, ("kx", "real"))
    low_forcing = jnp.dot(summed / realizations, backward, precision=highest)
    forcing = nonlinear * high_mask[None, None, :, None, None]
    forcing = (
        forcing + jnp.einsum("jm,cjyk->cmyk", low_select, low_forcing, precision=highest)[:, None]
    )
    forcing = forcing * column_mask[None, None, :, None, :]
    updated = current + dt_step * forcing
    slotted = jnp.take(
        updated.reshape(components, reals_dev, band_modes, rows_ht, kz_modes, 2), owner_map, axis=4
    )
    outgoing = slotted.reshape(components, reals_dev, band_modes, rows_ht, owners, slots_dev, 2)
    outgoing = outgoing.transpose(0, 1, 2, 4, 5, 6, 3)
    flat_out = outgoing.reshape(components, reals_dev, band_modes, owners, width_out)
    applied = apply_inverse(
        lax.all_to_all(flat_out, ("kx", "ht"), split_axis=3, concat_axis=3, tiled=True),
        helmholtz,
        kx_count,
        ht_count,
        slots_dev,
        rows_ht,
    )
    returned = lax.all_to_all(applied, ("kx", "ht"), split_axis=3, concat_axis=3, tiled=True)
    restored = returned.reshape(components, reals_dev, band_modes, owners, slots_dev, 2, rows_ht)
    restored = restored.transpose(0, 1, 2, 6, 3, 4, 5).reshape(
        components, reals_dev, band_modes, rows_ht, kz_modes, 2
    )
    current = jnp.take(restored, inverse_map, axis=4).reshape(
        components, reals_dev, band_modes, rows_ht, columns
    )
    return current


def solution(mesh):
    in_specs = (
        P(None, "real", "kx", "ht", None),
        P(),
        P("kx", None),
        P(),
        P("kx"),
        P(("kx", "ht"), None, None),
    )
    out_specs = P(None, "real", "kx", "ht", None)
    return jax.shard_map(local, mesh=mesh, in_specs=in_specs, out_specs=out_specs, check_vma=False)
```

profile of v0, /device:TPU:1, one launch (start us, length us, event | category | flops | bytes accessed | tf_op | source)
XLA Modules:
  0.0 327.1 jit_solution(15920989410416831472)
XLA Ops:
  6.6 2.4 fusion.12
  9.0 2.5 collective-permute-start
  11.5 4.0 %collective-permute-start.1 = (f32[3,1,4,64,256]{4,3,2,0,1:T(8,128)S(1)}, f32[3,1,4,64,256]{4,3,2,0,1:T(8,128)}, u32[]{:S(2)}, u32[]{:S(2)}) collective-permute-start(f32[3,1,4,64,256]{4,3,2,0,1:T(8,128)S(1)} %bitcast.259), channel_id=1, source_target_pairs={{32,0},{64,32},{96,64},{128,96},{160,128},{192,160},{224,192},{0,2... | collective-permute-start | bytes 2359304 | tf_op jit(solution)/shard_map/ppermute | solution.py:18
  15.6 3.1 convolution_bitcast_fusion
  19.8 12.9 %collective-permute-done = f32[3,1,4,64,256]{4,3,2,0,1:T(8,128)S(1)} collective-permute-done((f32[3,1,4,64,256]{4,3,2,0,1:T(8,128)S(1)}, f32[3,1,4,64,256]{4,3,2,0,1:T(8,128)S(1)}, u32[]{:S(2)}, u32[]{:S(2)}) %collective-permute-start) | collective-permute-done | bytes 786464 | tf_op jit(solution)/shard_map/ppermute | solution.py:15
  33.6 1.8 maximum_bitcast_fusion
  35.4 1.6 gather_fusion.7
  37.0 1.5 gather_fusion.5
  38.5 1.5 gather_fusion.4
  40.0 1.5 gather_fusion.3
  41.5 1.5 gather_fusion.2
  43.0 1.5 gather_fusion.1
  46.0 1.5 gather_fusion.6
  55.4 3.9 %stack.35 = f32[3,8,64,256]{3,1,2,0:T(8,128)} concatenate(f32[3,1,64,256]{3,1,2,0:T(1,128)S(1)} %stack.27, f32[3,1,64,256]{3,1,2,0:T(1,128)S(1)} %stack.28, f32[3,1,64,256]{3,1,2,0:T(1,128)S(1)} %stack.29, f32[3,1,64,256]{3,1,2,0:T(1,128)S(1)} %stack.30, f32[3,1,64,256]{3,1,2,0:T(1,128)S(1)} %stack.31, f32[3,1,64,256]{3,1,2,0:T(1,128)S(1)} %stack.32, ...), dimensions={1} | concatenate | bytes 3145728 | tf_op jit(solution)/shard_map/stack | solution.py:89
  60.4 35.1 %all-reduce.3.cloned.1.call-done = f32[3,1,8,64,256]{4,2,3,0,1:T(8,128)} async-done(((f32[3,1,8,64,256]{4,2,3,0,1:T(8,128)}), f32[3,1,8,64,256]{4,2,3,0,1:T(8,128)}) %all-reduce.3.cloned.1.call-update) | async-done | bytes 1572880 | tf_op jit(solution)/shard_map/psum | solution.py:80
  95.5 7.7 %fusion.51 = (f32[3,1,1,64,256]{4,2,3,0,1:T(1,128)S(1)}, f32[3,1,1,64,256]{4,2,3,0,1:T(1,128)S(1)}, f32[3,1,1,64,256]{4,2,3,0,1:T(1,128)S(1)}, f32[3,1,1,64,256]...) fusion(f32[3,1,8,64,256]{4,2,3,0,1:T(8,128)} %all-reduce.3.clon, ...), kind=kLoop, calls=%fused_computation.172 | loop fusion | bytes 3145728 | tf_op jit(solution)/shard_map/slice | solution.py:85
  108.7 3.5 %fusion.52 = (f32[1,1,1,64,256]{4,2,3,0,1:T(1,128)S(1)}, f32[1,1,1,64,256]{4,2,3,0,1:T(1,128)S(1)}, f32[1,1,1,64,256]{4,2,3,0,1:T(1,128)S(1)}, f32[1,1,1,64,256]...) fusion(f32[3,1,8,64,256]{4,2,3,0,1:T(8,128)} %all-reduce.3.clon, ...), kind=kLoop, calls=%fused_computation.173 | loop fusion | bytes 1048576 | tf_op jit(solution)/shard_map/slice | solution.py:86
  116.0 133.7 %all-reduce.5.cloned.1.call-done = f32[3,8,64,256]{3,1,2,0:T(8,128)} async-done(((f32[3,8,64,256]{3,1,2,0:T(8,128)}), f32[3,8,64,256]{3,1,2,0:T(8,128)}) %all-reduce.5.cloned.1.call-update) | async-done | bytes 1572880 | tf_op jit(solution)/shard_map/psum | solution.py:91
  249.7 3.5 %fusion = f32[3,8,64,128]{3,1,2,0:T(8,128)S(1)} fusion(f32[3,8,64,256]{3,1,2,0:T(8,128)} %all-reduce.5.cloned.1.call-done, f32[256]{0:T(256)S(1)} %convert_multiply_fusion, f32[128]{0:T(128)} %copy-done.17, pred[128]{0:T(512)(128)(4,1)S(1)} %fusion.42), kind=kOutput, calls=%fused_computation.12 | convolution fusion | flops 604504064 | bytes 2360960 | tf_op jit(solution)/shard_map/dot_general | solution.py:92
  254.4 5.9 %fusion.6 = f32[3,1,4,64,128]{4,3,2,0,1:T(8,128)} fusion(f32[3,1,4,64,128]{4,3,2,1,0:T(8,128)S(1)} %copy-done.14, f32[3,64,128,4]{2,3,1,0:T(4,128)S(1)} %fusion.50, f32[4,128]{1,0:T(4,128)S(1)} %compare_convert_fusion.1, f32[4]{0:T(128)} %copy-done.27, f32[256]{0:T(256)S(1)} %convert_multiply_fusion, f32[128]{0:T(128)} %copy-done.17, ...), kind=kOutput, calls=%fused_computation.21 | convolution fusion | flops 310280192 | bytes 11669168 | tf_op jit(solution)/shard_map/dot_general | solution.py:90
  264.4 27.5 %all_to_all.10 = f32[3,1,4,64,128]{4,2,0,1,3:T(4,128)S(1)} all-to-all(f32[3,1,4,64,128]{4,2,0,1,3:T(4,128)S(1)} %reshape.457), channel_id=1, replica_groups=mesh['kx'=8,'ht'=8,'real'=4] {'kx','ht'}, dimensions={3} | all-to-all | bytes 786432 | tf_op jit(solution)/shard_map/all_to_all | solution.py:106
  292.8 1.5 convolution_bitcast_fusion.1
  296.2 5.4 %all-to-all-start.1 = ((f32[3,1,4,64,128]{4,2,0,1,3:T(4,128)}), f32[3,1,4,64,128]{4,2,0,1,3:T(4,128)S(1)}, u32[]{:S(2)}, u32[]{:S(2)}) async-start(f32[3,1,4,64,128]{4,2,0,1,3:T(4,128)} %reshape.459), calls=%async_computation.1 | async-start | bytes 786432 | tf_op jit(solution)/shard_map/all_to_all | solution.py:113
  302.6 14.2 %all-to-all-done.1 = f32[3,1,4,64,128]{4,2,0,1,3:T(4,128)S(1)} async-done(((f32[3,1,4,64,128]{4,2,0,1,3:T(4,128)}), f32[3,1,4,64,128]{4,2,0,1,3:T(4,128)S(1)}, u32[]{:S(2)}, u32[]{:S(2)}) %all-to-all-start.1) | async-done | bytes 393248 | tf_op jit(solution)/shard_map/all_to_all | solution.py:113
  (169 shorter events, 33.5 us)
Async XLA Ops:
  6.5 286.2 %copy-start = (f32[1,512,512]{2,1,0:T(8,128)S(1)}, f32[1,512,512]{2,1,0:T(8,128)}, u32[]{:S(2)}) copy-start(f32[1,512,512]{2,1,0:T(8,128)} %param.15) | copy-start | bytes 3145732
  6.5 89.0 %all-reduce.3.cloned.1.call-start = ((), (), s32[]{:S(2)}) async-start(), calls=%async_computation.2 | async-start | bytes 3145728 | tf_op jit(solution)/shard_map/psum | solution.py:80
  6.6 12.2 %copy-start.17 = (f32[128]{0:T(128)}, f32[128]{0:T(128)S(1)}, u32[]{:S(2)}) copy-start(f32[128]{0:T(128)S(1)} %fusion.45) | copy-start | bytes 1540
  6.6 12.2 %copy-start.28 = (s32[4,8]{1,0:T(4,128)S(1)}, s32[4,8]{1,0:T(4,128)}, u32[]{:S(2)}) copy-start(s32[4,8]{1,0:T(4,128)} %param.12) | copy-start | bytes 388
  6.6 13.0 %copy-start.29 = (s32[8]{0:T(128)S(1)}, s32[8]{0:T(128)}, u32[]{:S(2)}) copy-start(s32[8]{0:T(128)} %param.11) | copy-start | bytes 100
  9.0 23.7 %copy-start.1 = (f32[256,3,4,64]{0,3,2,1:T(8,128)}, f32[256,3,4,64]{0,3,2,1:T(8,128)S(1)}, u32[]{:S(2)}) copy-start(f32[256,3,4,64]{0,3,2,1:T(8,128)S(1)} %fusion.12) | copy-start | bytes 2359300
  9.0 23.7 %collective-permute-start = (f32[3,1,4,64,256]{4,3,2,0,1:T(8,128)S(1)}, f32[3,1,4,64,256]{4,3,2,0,1:T(8,128)S(1)}, u32[]{:S(2)}, u32[]{:S(2)}) collective-permute-start(f32[3,1,4,64,256]{4,3,2,0,1:T(8,128)S(1)} %bitcast.258), channel_id=1, source_target_pairs={{0,32},{32,64},{64,96},{96,128},{128,160},{160,192},{192,224},{224... | collective-permute-start | bytes 2359304 | tf_op jit(solution)/shard_map/ppermute | solution.py:15
  11.5 22.1 %collective-permute-start.1 = (f32[3,1,4,64,256]{4,3,2,0,1:T(8,128)S(1)}, f32[3,1,4,64,256]{4,3,2,0,1:T(8,128)}, u32[]{:S(2)}, u32[]{:S(2)}) collective-permute-start(f32[3,1,4,64,256]{4,3,2,0,1:T(8,128)S(1)} %bitcast.259), channel_id=1, source_target_pairs={{32,0},{64,32},{96,64},{128,96},{160,128},{192,160},{224,192},{0,2... | collective-permute-start | bytes 2359304 | tf_op jit(solution)/shard_map/ppermute | solution.py:18
  15.6 19.9 %copy-start.18 = (s32[4]{0:T(128)}, s32[4]{0:T(128)S(1)}, u32[]{:S(2)}) copy-start(s32[4]{0:T(128)S(1)} %get-tuple-element.70) | copy-start | bytes 52
  18.8 230.9 %all-reduce.5.cloned.1.call-start = ((), (), s32[]{:S(2)}) async-start(), calls=%async_computation.3 | async-start | bytes 3145728 | tf_op jit(solution)/shard_map/psum | solution.py:91
  19.2 28.2 %copy-start.19 = (pred[4]{0:T(512)(128)(4,1)}, pred[4]{0:T(512)(128)(4,1)S(1)}, u32[]{:S(2)}) copy-start(pred[4]{0:T(512)(128)(4,1)S(1)} %compare_and_fusion.2) | copy-start | bytes 16
  19.3 29.6 %copy-start.20 = (pred[4]{0:T(512)(128)(4,1)}, pred[4]{0:T(512)(128)(4,1)S(1)}, u32[]{:S(2)}) copy-start(pred[4]{0:T(512)(128)(4,1)S(1)} %compare_and_fusion.4) | copy-start | bytes 16
  19.3 30.9 %copy-start.21 = (pred[4]{0:T(512)(128)(4,1)}, pred[4]{0:T(512)(128)(4,1)S(1)}, u32[]{:S(2)}) copy-start(pred[4]{0:T(512)(128)(4,1)S(1)} %compare_and_fusion.5) | copy-start | bytes 16
  19.3 31.1 %copy-start.22 = (pred[4]{0:T(512)(128)(4,1)}, pred[4]{0:T(512)(128)(4,1)S(1)}, u32[]{:S(2)}) copy-start(pred[4]{0:T(512)(128)(4,1)S(1)} %compare_and_fusion.6) | copy-start | bytes 16
  19.4 31.2 %copy-start.23 = (pred[4]{0:T(512)(128)(4,1)}, pred[4]{0:T(512)(128)(4,1)S(1)}, u32[]{:S(2)}) copy-start(pred[4]{0:T(512)(128)(4,1)S(1)} %compare_and_fusion.7) | copy-start | bytes 16
  19.4 31.4 %copy-start.24 = (pred[4]{0:T(512)(128)(4,1)}, pred[4]{0:T(512)(128)(4,1)S(1)}, u32[]{:S(2)}) copy-start(pred[4]{0:T(512)(128)(4,1)S(1)} %compare_and_fusion.8) | copy-start | bytes 16
  19.7 31.8 %copy-start.25 = (pred[4]{0:T(512)(128)(4,1)}, pred[4]{0:T(512)(128)(4,1)S(1)}, u32[]{:S(2)}) copy-start(pred[4]{0:T(512)(128)(4,1)S(1)} %compare_and_fusion.9) | copy-start | bytes 16
  19.8 32.1 %copy-start.26 = (pred[4]{0:T(512)(128)(4,1)}, pred[4]{0:T(512)(128)(4,1)S(1)}, u32[]{:S(2)}) copy-start(pred[4]{0:T(512)(128)(4,1)S(1)} %compare_and_fusion.3) | copy-start | bytes 16
  19.8 32.3 %copy-start.27 = (f32[4]{0:T(128)}, f32[4]{0:T(128)S(1)}, u32[]{:S(2)}) copy-start(f32[4]{0:T(128)S(1)} %broadcast_subtract_fusion) | copy-start | bytes 52
  55.4 5.0 %copy-start.32 = (s32[4]{0:T(128)S(1)}, s32[4]{0:T(128)}, u32[]{:S(2)}) copy-start(s32[4]{0:T(128)} %param.14) | copy-start | bytes 52
  112.2 142.2 %copy-start.3 = (f32[4,3,64,256]{3,2,1,0:T(8,128)S(1)}, f32[4,3,64,256]{3,2,1,0:T(8,128)}, u32[]{:S(2)}) copy-start(f32[4,3,64,256]{3,2,1,0:T(8,128)} %gather_fusion.7) | copy-start | bytes 2359300
  112.2 142.2 %copy-start.4 = (f32[4,3,64,256]{3,2,1,0:T(8,128)S(1)}, f32[4,3,64,256]{3,2,1,0:T(8,128)}, u32[]{:S(2)}) copy-start(f32[4,3,64,256]{3,2,1,0:T(8,128)} %gather_fusion.5) | copy-start | bytes 2359300
  249.7 4.7 %copy-start.15 = (f32[4,64,256]{2,1,0:T(8,128)S(1)}, f32[4,64,256]{2,1,0:T(8,128)}, u32[]{:S(2)}) copy-start(f32[4,64,256]{2,1,0:T(8,128)} %get-tuple-element.40) | copy-start | bytes 786436
  296.2 20.6 %all-to-all-start.1 = ((f32[3,1,4,64,128]{4,2,0,1,3:T(4,128)}), f32[3,1,4,64,128]{4,2,0,1,3:T(4,128)S(1)}, u32[]{:S(2)}, u32[]{:S(2)}) async-start(f32[3,1,4,64,128]{4,2,0,1,3:T(4,128)} %reshape.459), calls=%async_computation.1 | async-start | bytes 786432 | tf_op jit(solution)/shard_map/all_to_all | solution.py:113
  (15 other events, 38.1 us)
Sparse Core Ops, SparseCore 0:
  18.9 76.5 all-reduce.2
  98.9 150.7 all-reduce.4
where the time goes:
time: 328 us; the launch traced here: 327 us
  waiting for transfers between devices  196 us (60%)
  local copies, waits for them, and re-layouts  50.8 us (15%)
  blocking collectives  27.5 us (8%)
  matrix products  17.6 us (5%)
  between operations  14.4 us (4%)
  starting transfers between devices  12.1 us (4%)
  other arithmetic  8.77 us (3%)
    psum x1, waiting for transfers between devices, local(): summed = lax.psum(stress, ('kx', 'real'))  134 us
    psum x1, waiting for transfers between devices, local(): low_fields = lax.psum(own_low, 'kx')  35.1 us
    all_to_all x1, blocking collectives, local(): lax.all_to_all(flat_out, ('kx', 'ht'), split_axis=3, concat_axis=3, tiled...  27.5 us
    all_to_all x1, waiting for transfers between devices, local(): lax.all_to_all(applied, ('kx', 'ht'), split_axis=3, concat_axis=3, tiled=...  14.2 us
    ppermute x1, waiting for transfers between devices, extended_2(): lax.ppermute(lax.slice_in_dim(block, block.shape[dim] - width, None, axis...  12.9 us
    gather x8, local copies, waits for them, and re-layouts, local(): partner = jnp.take(extended, local_partner[:, member], axis=2)  12 us
    unnamed x84, local copies, waits for them, and re-layouts  11.8 us
    slice x1, local copies, waits for them, and re-layouts, local(): low_one = low_fields[:, :, member:member + 1]  7.67 us
  transfers between devices with their start and end apart: 5, of which 4 were waited for; matrix products, arithmetic and copies ran while one was open for 15% of the time, Pallas kernels for 0%

commit v1 on v0

v1 whole, which is shorter than its diff:
```python
import functools

import jax
import jax.numpy as jnp
import numpy as np
from jax import lax
from jax.experimental import pallas as pl
from jax.experimental.pallas import tpu as pltpu
from jax.sharding import PartitionSpec as P

MESH = pl.DeviceIdType.MESH
F32 = jnp.float32
BF16 = jnp.bfloat16

dt_step = 0.1
COMP, BAND, ROWS, COLS = 3, 4, 64, 128
NKX, NHT, NREAL = 8, 8, 4
MODES, LOW, POINTS, HEIGHTS, SLOTS = 32, 8, 256, 512, 64
ORDER = (1, 0, 2)


def spanwise_tables():
    ids = np.arange(COLS)
    wave = (ids // 2).astype(np.float32)
    spots = np.float32(2.0 * np.pi) * np.arange(POINTS).astype(np.float32) / np.float32(POINTS)
    phases = (wave[:, None] * spots[None, :]).astype(np.float64)
    forward = np.where(ids[:, None] % 2 == 0, np.cos(phases), -np.sin(phases)) / 8.0
    forward = forward.astype(np.float32)
    backward = np.ascontiguousarray(forward.T) * np.float32(0.5)

    def halves(table):
        head = table.astype(BF16)
        return head, (table - head.astype(np.float32)).astype(BF16)

    return (*halves(forward), *halves(backward))


def split(x):
    head = x.astype(BF16)
    return head, (x - head.astype(F32)).astype(BF16)


def mm(a, b):
    return lax.dot_general(a, b, (((1,), (0,)), ((), ())), preferred_element_type=F32)


def mm_nt(a, b):
    return lax.dot_general(a, b, (((1,), (1,)), ((), ())), preferred_element_type=F32)


def mm3(x, head, tail):
    hi, lo = split(x)
    return mm(hi, head) + (mm(hi, tail) + mm(lo, head))


def kernel(
    v, low_s, nb_own, omap_s, cnt_own, helm, t_fh, t_fl, t_bh, t_bl,
    out,
    vr, phys, hl, nl, upd, snd, ubuf, wsnd, rbuf, strs, zlow, onehot, oh, oht, hf, hth, htl,
    fh, fl, bh, bl, nb_s, cnt_s, inv_s,
    a_send, a_recv, i_send, i_recv, st_send, st_recv, b_send, b_recv, c_send, c_recv, l_sem,
):
    kx, ht, re = lax.axis_index("kx"), lax.axis_index("ht"), lax.axis_index("real")
    slot = kx * NHT + ht
    source = ht * NKX + kx

    barrier = pltpu.get_barrier_semaphore()
    for d in range(1, NKX):
        pl.semaphore_signal(barrier, 1, device_id=(lax.rem(kx + d, NKX), ht, re), device_id_type=MESH)
    for d in range(1, NHT):
        pl.semaphore_signal(barrier, 1, device_id=(kx, lax.rem(ht + d, NHT), re), device_id_type=MESH)
    for d in range(1, NREAL):
        pl.semaphore_signal(barrier, 1, device_id=(kx, ht, lax.rem(re + d, NREAL)), device_id_type=MESH)

    local = [
        pltpu.make_async_copy(src, dst, l_sem.at[i])
        for i, (src, dst) in enumerate(
            ((helm.at[0], hf), (t_fh, fh), (t_fl, fl), (t_bh, bh), (t_bl, bl))
        )
    ]
    for copy in local:
        copy.start()
    for i, c in enumerate(ORDER):
        for a in range(2):
            pltpu.make_async_copy(
                v.at[c, 0, :, pl.ds(a * 32 + kx * 4, 4), :],
                vr.at[c, pl.ds(kx * BAND, BAND), pl.ds(a * 4, 4), :],
                a_recv.at[c],
            ).start()
    pltpu.make_async_copy(nb_own, nb_s.at[kx], i_recv.at[0]).start()
    pltpu.make_async_copy(cnt_own, cnt_s.at[kx], i_recv.at[1]).start()

    pl.semaphore_wait(barrier, (NKX - 1) + (NHT - 1) + (NREAL - 1))

    for d in range(1, NKX):
        peer = lax.rem(kx + d, NKX)
        for own, table, i in ((nb_own, nb_s, 0), (cnt_own, cnt_s, 1)):
            pltpu.make_async_remote_copy(
                own, table.at[kx], i_send.at[i], i_recv.at[i], device_id=(peer, ht, re), device_id_type=MESH
            ).start()
    for c in ORDER:
        for d in (4, 3, 5, 2, 6, 1, 7):
            peer = lax.rem(kx + d, NKX)
            for a in range(2):
                pltpu.make_async_remote_copy(
                    v.at[c, 0, :, pl.ds(a * 32 + peer * 4, 4), :],
                    vr.at[c, pl.ds(kx * BAND, BAND), pl.ds(a * 4, 4), :],
                    a_send.at[c],
                    a_recv.at[c],
                    device_id=(peer, ht, re),
                    device_id_type=MESH,
                ).start()

    lane = lax.broadcasted_iota(jnp.int32, (1, COLS), 1)

    def one_row(s, _):
        for p in range(2):
            onehot[pl.ds(p * SLOTS + s, 1), :] = (lane == 2 * omap_s[s] + p).astype(F32)
        return 0

    lax.fori_loop(0, SLOTS, one_row, 0)
    square = onehot[...]
    oh[...] = square.astype(BF16)
    oht[...] = square.T.astype(BF16)

    def one_mode(m, _):
        place = jnp.int32(LOW)
        for j in range(LOW):
            place = jnp.where(low_s[j] == m, jnp.int32(j), place)
        inv_s[m] = place
        return 0

    lax.fori_loop(0, MODES, one_mode, 0)
    for c in range(COMP):
        zlow[c, LOW] = jnp.zeros((8, COLS), F32)
    for copy in local:
        copy.wait()
    for i in range(4):
        for j in range(4):
            block = hf[pl.ds(i * 128, 128), pl.ds(j * 128, 128)].T
            head, tail = split(block)
            hth[pl.ds(j * 128, 128), pl.ds(i * 128, 128)] = head
            htl[pl.ds(j * 128, 128), pl.ds(i * 128, 128)] = tail
    pltpu.make_async_copy(nb_s, nb_s, i_recv.at[0]).wait()
    pltpu.make_async_copy(cnt_s, cnt_s, i_recv.at[1]).wait()

    def products(c):
        pltpu.make_async_copy(vr.at[c], vr.at[c], a_recv.at[c]).wait()
        fields = vr[c].reshape(MODES * 8, COLS)
        phys[c] = mm3(fields, fh[...], fl[...]).reshape(MODES, 8, POINTS)
        sums = []
        for half in range(2):
            part = pl.ds(half * 128, 128)
            low_1 = [phys[1, low_s[j], :, part] for j in range(LOW)]
            low_c = low_1 if c == 1 else [phys[c, low_s[j], :, part] for j in range(LOW)]

            def one(m, sums, part=part, low_1=low_1, low_c=low_c):
                high = (inv_s[m] == LOW).astype(F32)
                mine = phys[c, m, :, part] * high
                band, row = m // BAND, lax.rem(m, BAND)
                total = jnp.zeros((8, 128), F32)
                new = []
                for j in range(LOW):
                    near = nb_s[band, row, j]
                    p_1 = phys[1, near, :, part]
                    if c == 1:
                        total = total + low_1[j] * p_1
                    else:
                        total = total + (low_c[j] * p_1 + phys[c, near, :, part] * low_1[j])
                    new.append(sums[j] + mine * p_1)
                if c == 1:
                    total = total + total
                hl[m, :, part] = total * high
                return tuple(new)

            sums.append(lax.fori_loop(0, MODES, one, tuple(jnp.zeros((8, 128), F32) for _ in range(LOW))))
        stress = jnp.concatenate(
            [jnp.concatenate([sums[0][j], sums[1][j]], axis=1) for j in range(LOW)], axis=0
        )
        strs[re, c] = mm3(stress * (1.0 / NREAL), bh[...], bl[...])
        for d in range(1, NREAL):
            pltpu.make_async_remote_copy(
                strs.at[re, c],
                strs.at[re, c],
                st_send.at[c],
                st_recv.at[c],
                device_id=(kx, ht, lax.rem(re + d, NREAL)),
                device_id_type=MESH,
            ).start()
        nl[c] = mm3(hl[...].reshape(MODES * 8, POINTS), bh[...], bl[...]).reshape(MODES, 8, COLS)

    def forced(c):
        pltpu.make_async_copy(strs.at[pl.ds(0, 3), 0], strs.at[pl.ds(0, 3), 0], st_recv.at[c]).wait()
        summed = (strs[0, c] + strs[1, c]) + (strs[2, c] + strs[3, c])
        zlow[c, pl.ds(0, LOW)] = summed.reshape(LOW, 8, COLS)
        half_lane = lax.broadcasted_iota(jnp.int32, (8, COLS), 1) // 2

        def one(m, _):
            gain = jnp.where(half_lane < cnt_s[m // BAND, lax.rem(m, BAND)], F32(dt_step), F32(0.0))
            upd[pl.ds(m * 8, 8), :] = vr[c, m] + gain * (nl[c, m] + zlow[c, inv_s[m]])
            return 0

        lax.fori_loop(0, MODES, one, 0)
        rows = [
            upd[pl.ds(a * 4 + 2 * tile + y, MODES, stride=8), :]
            for tile in range(2)
            for a in range(2)
            for y in range(2)
        ]
        hi, lo = split(jnp.concatenate(rows, axis=0))
        turned = mm_nt(oh[...], hi) + mm_nt(oh[...], lo)
        odd = (lax.broadcasted_iota(jnp.int32, (SLOTS, 128), 1) // 32) % 2 == 1
        for tile in range(2):
            even_p = turned[:SLOTS, tile * 128 : tile * 128 + 128]
            odd_p = turned[SLOTS:, tile * 128 : tile * 128 + 128]
            first = jnp.where(odd, pltpu.roll(odd_p, 32, 1), even_p)
            second = jnp.where(odd, odd_p, pltpu.roll(even_p, 96, 1))
            snd[c, pl.ds(2 * tile, SLOTS, stride=4), :] = first
            snd[c, pl.ds(2 * tile + 1, SLOTS, stride=4), :] = second
        pltpu.make_async_copy(
            snd.at[c, pl.ds(slot * 4, 4), :], ubuf.at[c, pl.ds(source * 4, 4), :], b_recv.at[c]
        ).start()

        def send(t, _):
            to_kx, to_ht = lax.rem(kx + lax.rem(t, NKX), NKX), lax.rem(ht + t // NKX, NHT)
            pltpu.make_async_remote_copy(
                snd.at[c, pl.ds((to_kx * NHT + to_ht) * 4, 4), :],
                ubuf.at[c, pl.ds(source * 4, 4), :],
                b_send.at[c],
                b_recv.at[c],
                device_id=(to_kx, to_ht, re),
                device_id_type=MESH,
            ).start()
            return 0

        lax.fori_loop(1, SLOTS, send, 0)

    first_half = lax.broadcasted_iota(jnp.int32, (MODES, 128), 1) < 64

    def solved(c):
        pltpu.make_async_copy(ubuf.at[c], ubuf.at[c], b_recv.at[c]).wait()
        given = ubuf[c]
        swapped = pltpu.roll(given, 64, 1)
        pieces = []
        for block in range(NHT):
            pieces += [given[block * 32 : block * 32 + 32], swapped[block * 32 : block * 32 + 32]]
        fields = jnp.concatenate(pieces, axis=0).T[:64]
        answer = mm3(fields, hth[...], htl[...])
        for tile in range(4):
            even_p = answer[:MODES, tile * 128 : tile * 128 + 128]
            odd_p = answer[MODES:, tile * 128 : tile * 128 + 128]
            wsnd[c, pl.ds((2 * tile) * MODES, MODES), :] = jnp.where(
                first_half, even_p, pltpu.roll(odd_p, 64, 1)
            )
            wsnd[c, pl.ds((2 * tile + 1) * MODES, MODES), :] = jnp.where(
                first_half, pltpu.roll(even_p, 64, 1), odd_p
            )
        pltpu.make_async_copy(
            wsnd.at[c, pl.ds(ht * MODES + kx * 4, 4), :], rbuf.at[c, pl.ds(slot * 4, 4), :], c_recv.at[c]
        ).start()

        def send(t, _):
            to_kx, to_ht = lax.rem(kx + lax.rem(t, NKX), NKX), lax.rem(ht + t // NKX, NHT)
            pltpu.make_async_remote_copy(
                wsnd.at[c, pl.ds(to_ht * MODES + to_kx * 4, 4), :],
                rbuf.at[c, pl.ds(slot * 4, 4), :],
                c_send.at[c],
                c_recv.at[c],
                device_id=(to_kx, to_ht, re),
                device_id_type=MESH,
            ).start()
            return 0

        lax.fori_loop(1, SLOTS, send, 0)

    def placed(c):
        pltpu.make_async_copy(rbuf.at[c], rbuf.at[c], c_recv.at[c]).wait()
        low_half = lax.broadcasted_iota(jnp.int32, (SLOTS, 128), 1) < 64
        columns = []
        for pair in range(2):
            one = rbuf[c, pl.ds(2 * pair, SLOTS, stride=4), :]
            two = rbuf[c, pl.ds(2 * pair + 1, SLOTS, stride=4), :]
            columns.append(
                jnp.concatenate(
                    [
                        jnp.where(low_half, one, pltpu.roll(two, 64, 1)),
                        jnp.where(low_half, pltpu.roll(one, 64, 1), two),
                    ],
                    axis=0,
                )
            )
        hi, lo = split(jnp.concatenate(columns, axis=1))
        back = mm(oht[...], hi) + mm(oht[...], lo)
        for pair in range(2):
            out[c, 0, pl.ds(2 * pair, 2), :, :] = back[:, pair * 128 : pair * 128 + 128].T.reshape(2, ROWS, COLS)

    products(1)
    products(0)
    forced(1)
    products(2)
    forced(0)
    forced(2)
    for c in ORDER:
        solved(c)
    for c in ORDER:
        placed(c)

    pltpu.make_async_copy(nb_s.at[pl.ds(0, 7)], nb_s.at[pl.ds(0, 7)], i_send.at[0]).wait()
    pltpu.make_async_copy(cnt_s.at[pl.ds(0, 7)], cnt_s.at[pl.ds(0, 7)], i_send.at[1]).wait()
    for c in range(COMP):
        sent = vr.at[c, pl.ds(0, MODES - BAND)]
        pltpu.make_async_copy(sent, sent, a_send.at[c]).wait()
        sent = strs.at[pl.ds(0, NREAL - 1), c]
        pltpu.make_async_copy(sent, sent, st_send.at[c]).wait()
        sent = snd.at[c, pl.ds(0, 252), :]
        pltpu.make_async_copy(sent, sent, b_send.at[c]).wait()
        sent = wsnd.at[c, pl.ds(0, 252), :]
        pltpu.make_async_copy(sent, sent, c_send.at[c]).wait()


def local(velocity, low_index, neighbours, owner_map, mode_counts, helmholtz):
    tables = [jnp.asarray(t) for t in spanwise_tables()]
    hbm = pl.BlockSpec(memory_space=pl.ANY)
    smem = pl.BlockSpec(memory_space=pltpu.SMEM)
    vmem = pl.BlockSpec(memory_space=pltpu.VMEM)
    dma = pltpu.SemaphoreType.DMA
    return pl.pallas_call(
        kernel,
        out_shape=jax.ShapeDtypeStruct(velocity.shape, F32),
        in_specs=[hbm, smem, hbm, smem, hbm, hbm, hbm, hbm, hbm, hbm],
        out_specs=vmem,
        scratch_shapes=[
            pltpu.VMEM((COMP, MODES, 8, COLS), F32),
            pltpu.VMEM((COMP, MODES, 8, POINTS), F32),
            pltpu.VMEM((MODES, 8, POINTS), F32),
            pltpu.VMEM((COMP, MODES, 8, COLS), F32),
            pltpu.VMEM((MODES * 8, COLS), F32),
            pltpu.VMEM((COMP, 256, 128), F32),
            pltpu.VMEM((COMP, 256, 128), F32),
            pltpu.VMEM((COMP, 256, 128), F32),
            pltpu.VMEM((COMP, 256, 128), F32),
            pltpu.VMEM((NREAL, COMP, LOW * 8, COLS), F32),
            pltpu.VMEM((COMP, LOW + 1, 8, COLS), F32),
            pltpu.VMEM((128, COLS), F32),
            pltpu.VMEM((128, COLS), BF16),
            pltpu.VMEM((COLS, 128), BF16),
            pltpu.VMEM((HEIGHTS, HEIGHTS), F32),
            pltpu.VMEM((HEIGHTS, HEIGHTS), BF16),
            pltpu.VMEM((HEIGHTS, HEIGHTS), BF16),
            pltpu.VMEM((COLS, POINTS), BF16),
            pltpu.VMEM((COLS, POINTS), BF16),
            pltpu.VMEM((POINTS, COLS), BF16),
            pltpu.VMEM((POINTS, COLS), BF16),
            pltpu.SMEM((NKX, BAND, LOW), jnp.int32),
            pltpu.SMEM((NKX, BAND), jnp.int32),
            pltpu.SMEM((MODES,), jnp.int32),
            dma((COMP,)),
            dma((COMP,)),
            dma((2,)),
            dma((2,)),
            dma((COMP,)),
            dma((COMP,)),
            dma((COMP,)),
            dma((COMP,)),
            dma((COMP,)),
            dma((COMP,)),
            dma((5,)),
        ],
        compiler_params=pltpu.CompilerParams(collective_id=0, has_side_effects=True),
    )(velocity, low_index, neighbours, owner_map, mode_counts, helmholtz, *tables)


def solution(mesh):
    in_specs = (
        P(None, "real", "kx", "ht", None),
        P(),
        P("kx", None),
        P(),
        P("kx"),
        P(("kx", "ht"), None, None),
    )
    out_specs = P(None, "real", "kx", "ht", None)
    return jax.shard_map(local, mesh=mesh, in_specs=in_specs, out_specs=out_specs, check_vma=False)
```

time: 328 us -> 51.3 us (0.16)
  waiting for transfers between devices: 196 us -> 0 us
  Pallas kernels: 0 us -> 49.5 us
  local copies, waits for them, and re-layouts: 50.8 us -> 1.77 us
  blocking collectives: 27.5 us -> 0 us
  matrix products: 17.6 us -> 0 us
  between operations: 14.4 us -> 0.01 us
  starting transfers between devices: 12.1 us -> 0 us
  other arithmetic: 8.77 us -> 0 us
    psum x2 -> x0, waiting for transfers between devices: 169 us -> none  [the longest x1 134 us: local(): summed = lax.psum(stress, ('kx', 'real'))]
    pallas_call x0 -> x1, Pallas kernels: none -> 49.5 us  [local(): pl.pallas_call(kernel, out_shape=jax.ShapeDtypeStruct(velocity.shape, F32...]
    all_to_all x1 -> x0, blocking collectives: 27.5 us -> none  [local(): lax.all_to_all(flat_out, ('kx', 'ht'), split_axis=3, concat_axis=3, tiled...]
    dot_general x6 -> x0, matrix products: 17.6 us -> none  [the longest x1 5.87 us: local(): nonlinear = jnp.dot(high_low, backward, precision=highest)]
    all_to_all x1 -> x0, waiting for transfers between devices: 14.2 us -> none  [local(): lax.all_to_all(applied, ('kx', 'ht'), split_axis=3, concat_axis=3, tiled=...]
    gather x10 -> x0, local copies, waits for them, and re-layouts: 14.1 us -> none  [the longest x8 12 us: local(): partner = jnp.take(extended, local_partner[:, member], axis=2)]
    ppermute x2 -> x0, waiting for transfers between devices: 12.9 us -> none  [the longest x1 12.9 us: extended_2(): lax.ppermute(lax.slice_in_dim(block, block.shape[dim] - width, None, axis...]
    slice x3 -> x0, local copies, waits for them, and re-layouts: 11.4 us -> none  [the longest x1 7.67 us: local(): low_one = low_fields[:, :, member:member + 1]]
  transfers between devices with their start and end apart: 5 -> 0, of which waited for: 4 -> 0; matrix products, arithmetic and copies ran while one was open for 15% -> 0% of each run, Pallas kernels for 0% -> 0%
where the time goes in v1:
time: 51.3 us; the launch traced here: 51.2 us
  Pallas kernels  49.5 us (96%)
  local copies, waits for them, and re-layouts  1.77 us (3%)
    pallas_call x1, Pallas kernels, local(): pl.pallas_call(kernel, out_shape=jax.ShapeDtypeStruct(velocity.shape, F32...  49.5 us
    unnamed x1, local copies, waits for them, and re-layouts  1.77 us

profile of v1, /device:TPU:1, one launch (start us, length us, event | category | flops | bytes accessed | tf_op | source)
XLA Modules:
  0.0 51.2 jit_solution(8936988748999872791)
XLA Ops:
  0.0 49.5 %shard_map.100 = f32[3,1,4,64,128]{4,3,2,1,0:T(8,128)} custom-call(f32[3,1,4,64,128]{4,3,2,1,0:T(8,128)} %v.1, s32[8]{0:T(128)} %low_s.1, s32[4,8]{1,0:T(4,128)} %nb_own.1, s32[64]{0:T(128)} %omap_s.1, s32[4]{0:T(128)} %cnt_own.1, f32[1,512,512]{2,1,0:T(8,128)} %helm.1, bf16[128,256]{1,0:T(8,128)(2,1)} %constant.8.clone.t_fh, ...), custom_call_target="tpu_custom_call" | custom-call | tf_op jit(solution)/shard_map/pallas_call | solution.py:327
  49.5 1.8 %copy.12 = f32[3,1,4,64,128]{4,3,2,1,0:T(8,128)} copy(f32[3,1,4,64,128]{4,3,2,1,0:T(8,128)} %shard_map.100) | data formatting | bytes 786432

commit v2 on v1

--- a/solution.py
+++ b/solution.py
@@ -63,6 +63,8 @@
     kx, ht, re = lax.axis_index("kx"), lax.axis_index("ht"), lax.axis_index("real")
     slot = kx * NHT + ht
     source = ht * NKX + kx
+    kxs = [lax.rem(kx + d, NKX) for d in range(NKX)]
+    hts = [lax.rem(ht + d, NHT) for d in range(NHT)]
 
     barrier = pltpu.get_barrier_semaphore()
     for d in range(1, NKX):
@@ -148,35 +150,16 @@
         pltpu.make_async_copy(vr.at[c], vr.at[c], a_recv.at[c]).wait()
         fields = vr[c].reshape(MODES * 8, COLS)
         phys[c] = mm3(fields, fh[...], fl[...]).reshape(MODES, 8, POINTS)
-        sums = []
-        for half in range(2):
-            part = pl.ds(half * 128, 128)
-            low_1 = [phys[1, low_s[j], :, part] for j in range(LOW)]
-            low_c = low_1 if c == 1 else [phys[c, low_s[j], :, part] for j in range(LOW)]
-
-            def one(m, sums, part=part, low_1=low_1, low_c=low_c):
-                high = (inv_s[m] == LOW).astype(F32)
-                mine = phys[c, m, :, part] * high
-                band, row = m // BAND, lax.rem(m, BAND)
-                total = jnp.zeros((8, 128), F32)
-                new = []
+        def stress_band(band, sums):
+            sums = list(sums)
+            for row in range(BAND):
+                mine = phys[c, band * BAND + row] * (inv_s[band * BAND + row] == LOW).astype(F32)
                 for j in range(LOW):
-                    near = nb_s[band, row, j]
-                    p_1 = phys[1, near, :, part]
-                    if c == 1:
-                        total = total + low_1[j] * p_1
-                    else:
-                        total = total + (low_c[j] * p_1 + phys[c, near, :, part] * low_1[j])
-                    new.append(sums[j] + mine * p_1)
-                if c == 1:
-                    total = total + total
-                hl[m, :, part] = total * high
-                return tuple(new)
-
-            sums.append(lax.fori_loop(0, MODES, one, tuple(jnp.zeros((8, 128), F32) for _ in range(LOW))))
-        stress = jnp.concatenate(
-            [jnp.concatenate([sums[0][j], sums[1][j]], axis=1) for j in range(LOW)], axis=0
-        )
+                    sums[j] = sums[j] + mine * phys[1, nb_s[band, row, j]]
+            return tuple(sums)
+
+        zeros = tuple(jnp.zeros((8, POINTS), F32) for _ in range(LOW))
+        stress = jnp.concatenate(lax.fori_loop(0, NKX, stress_band, zeros), axis=0)
         strs[re, c] = mm3(stress * (1.0 / NREAL), bh[...], bl[...])
         for d in range(1, NREAL):
             pltpu.make_async_remote_copy(
@@ -187,6 +170,24 @@
                 device_id=(kx, ht, lax.rem(re + d, NREAL)),
                 device_id_type=MESH,
             ).start()
+        low_1 = [phys[1, low_s[j]] for j in range(LOW)]
+        low_c = low_1 if c == 1 else [phys[c, low_s[j]] for j in range(LOW)]
+
+        def high_band(band, _):
+            for row in range(BAND):
+                high = (inv_s[band * BAND + row] == LOW).astype(F32)
+                first, second = [], []
+                for j in range(LOW):
+                    near = nb_s[band, row, j]
+                    first.append(low_c[j] * phys[1, near])
+                    if c != 1:
+                        second.append(low_1[j] * phys[c, near])
+                total = functools.reduce(lambda a, b: a + b, first)
+                total = total + (total if c == 1 else functools.reduce(lambda a, b: a + b, second))
+                hl[band * BAND + row] = total * high
+            return 0
+
+        lax.fori_loop(0, NKX, high_band, 0)
         nl[c] = mm3(hl[...].reshape(MODES * 8, POINTS), bh[...], bl[...]).reshape(MODES, 8, COLS)
 
     def forced(c):
@@ -195,12 +196,14 @@
         zlow[c, pl.ds(0, LOW)] = summed.reshape(LOW, 8, COLS)
         half_lane = lax.broadcasted_iota(jnp.int32, (8, COLS), 1) // 2
 
-        def one(m, _):
-            gain = jnp.where(half_lane < cnt_s[m // BAND, lax.rem(m, BAND)], F32(dt_step), F32(0.0))
-            upd[pl.ds(m * 8, 8), :] = vr[c, m] + gain * (nl[c, m] + zlow[c, inv_s[m]])
+        def one_band(band, _):
+            for row in range(BAND):
+                m = band * BAND + row
+                gain = jnp.where(half_lane < cnt_s[band, row], F32(dt_step), F32(0.0))
+                upd[pl.ds(m * 8, 8), :] = vr[c, m] + gain * (nl[c, m] + zlow[c, inv_s[m]])
             return 0
 
-        lax.fori_loop(0, MODES, one, 0)
+        lax.fori_loop(0, NKX, one_band, 0)
         rows = [
             upd[pl.ds(a * 4 + 2 * tile + y, MODES, stride=8), :]
             for tile in range(2)
@@ -221,8 +224,8 @@
             snd.at[c, pl.ds(slot * 4, 4), :], ubuf.at[c, pl.ds(source * 4, 4), :], b_recv.at[c]
         ).start()
 
-        def send(t, _):
-            to_kx, to_ht = lax.rem(kx + lax.rem(t, NKX), NKX), lax.rem(ht + t // NKX, NHT)
+        for t in range(1, SLOTS):
+            to_kx, to_ht = kxs[t % NKX], hts[t // NKX]
             pltpu.make_async_remote_copy(
                 snd.at[c, pl.ds((to_kx * NHT + to_ht) * 4, 4), :],
                 ubuf.at[c, pl.ds(source * 4, 4), :],
@@ -231,9 +234,6 @@
                 device_id=(to_kx, to_ht, re),
                 device_id_type=MESH,
             ).start()
-            return 0
-
-        lax.fori_loop(1, SLOTS, send, 0)
 
     first_half = lax.broadcasted_iota(jnp.int32, (MODES, 128), 1) < 64
 
@@ -259,8 +259,8 @@
             wsnd.at[c, pl.ds(ht * MODES + kx * 4, 4), :], rbuf.at[c, pl.ds(slot * 4, 4), :], c_recv.at[c]
         ).start()
 
-        def send(t, _):
-            to_kx, to_ht = lax.rem(kx + lax.rem(t, NKX), NKX), lax.rem(ht + t // NKX, NHT)
+        for t in range(1, SLOTS):
+            to_kx, to_ht = kxs[t % NKX], hts[t // NKX]
             pltpu.make_async_remote_copy(
                 wsnd.at[c, pl.ds(to_ht * MODES + to_kx * 4, 4), :],
                 rbuf.at[c, pl.ds(slot * 4, 4), :],
@@ -269,9 +269,6 @@
                 device_id=(to_kx, to_ht, re),
                 device_id_type=MESH,
             ).start()
-            return 0
-
-        lax.fori_loop(1, SLOTS, send, 0)
 
     def placed(c):
         pltpu.make_async_copy(rbuf.at[c], rbuf.at[c], c_recv.at[c]).wait()
@@ -324,9 +321,9 @@
     smem = pl.BlockSpec(memory_space=pltpu.SMEM)
     vmem = pl.BlockSpec(memory_space=pltpu.VMEM)
     dma = pltpu.SemaphoreType.DMA
-    return pl.pallas_call(
+    held = pl.pallas_call(
         kernel,
-        out_shape=jax.ShapeDtypeStruct(velocity.shape, F32),
+        out_shape=pltpu.VMEM(velocity.shape, F32),
         in_specs=[hbm, smem, hbm, smem, hbm, hbm, hbm, hbm, hbm, hbm],
         out_specs=vmem,
         scratch_shapes=[
@@ -368,6 +365,7 @@
         ],
         compiler_params=pltpu.CompilerParams(collective_id=0, has_side_effects=True),
     )(velocity, low_index, neighbours, owner_map, mode_counts, helmholtz, *tables)
+    return held
 
 
 def solution(mesh):

time: 51.3 us -> 46.1 us (0.90)
  Pallas kernels: 49.5 us -> 45.2 us
  local copies, waits for them, and re-layouts: 1.77 us -> 0.75 us
    pallas_call x1, Pallas kernels: 49.5 us -> 45.2 us  [local(): pl.pallas_call(kernel, out_shape=pltpu.VMEM(velocity.shape, F32), in_spec...]
    unnamed x1, local copies, waits for them, and re-layouts: 1.77 us -> 0.75 us
where the time goes in v2:
time: 46.1 us; the launch traced here: 46 us
  Pallas kernels  45.2 us (98%)
  local copies, waits for them, and re-layouts  0.75 us (2%)
    pallas_call x1, Pallas kernels, local(): pl.pallas_call(kernel, out_shape=pltpu.VMEM(velocity.shape, F32), in_spec...  45.2 us

profile of v2, /device:TPU:1, one launch (start us, length us, event | category | flops | bytes accessed | tf_op | source)
XLA Modules:
  0.0 46.0 jit_solution(15857133510858734536)
XLA Ops:
  0.0 45.2 %shard_map.100 = f32[3,1,4,64,128]{4,3,2,1,0:T(8,128)S(1)} custom-call(f32[3,1,4,64,128]{4,3,2,1,0:T(8,128)} %v.1, s32[8]{0:T(128)} %low_s.1, s32[4,8]{1,0:T(4,128)} %nb_own.1, s32[64]{0:T(128)} %omap_s.1, s32[4]{0:T(128)} %cnt_own.1, f32[1,512,512]{2,1,0:T(8,128)} %helm.1, bf16[128,256]{1,0:T(8,128)(2,1)} %constant.8.clone.t_fh, ...), custom_call_target="tpu_custom_call" | custom-call | tf_op jit(solution)/shard_map/pallas_call | solution.py:324
  45.2 0.7 %copy.12 = f32[3,1,4,64,128]{4,3,2,1,0:T(8,128)} copy(f32[3,1,4,64,128]{4,3,2,1,0:T(8,128)S(1)} %shard_map.100) | data formatting | bytes 786432

commit v3 on v2

--- a/solution.py
+++ b/solution.py
@@ -13,26 +13,29 @@
 BF16 = jnp.bfloat16
 
 dt_step = 0.1
+
+
+def ring(step, count):
+    return min(step, count - step)
+
+
 COMP, BAND, ROWS, COLS = 3, 4, 64, 128
 NKX, NHT, NREAL = 8, 8, 4
 MODES, LOW, POINTS, HEIGHTS, SLOTS = 32, 8, 256, 512, 64
 ORDER = (1, 0, 2)
-
-
-def spanwise_tables():
+FAR_FIRST = (4, 3, 5, 2, 6, 1, 7)
+PAIRS = [(dk, dh) for dk in range(NKX) for dh in range(NHT) if dk + dh]
+PAIRS.sort(key=lambda p: (-ring(p[1] // 2, NHT // 2), -ring(p[0], NKX)))
+
+
+def forward_table():
     ids = np.arange(COLS)
     wave = (ids // 2).astype(np.float32)
     spots = np.float32(2.0 * np.pi) * np.arange(POINTS).astype(np.float32) / np.float32(POINTS)
     phases = (wave[:, None] * spots[None, :]).astype(np.float64)
-    forward = np.where(ids[:, None] % 2 == 0, np.cos(phases), -np.sin(phases)) / 8.0
-    forward = forward.astype(np.float32)
-    backward = np.ascontiguousarray(forward.T) * np.float32(0.5)
-
-    def halves(table):
-        head = table.astype(BF16)
-        return head, (table - head.astype(np.float32)).astype(BF16)
-
-    return (*halves(forward), *halves(backward))
+    forward = (np.where(ids[:, None] % 2 == 0, np.cos(phases), -np.sin(phases)) / 8.0).astype(np.float32)
+    head = forward.astype(BF16)
+    return np.stack([head, (forward - head.astype(np.float32)).astype(BF16)])
 
 
 def split(x):
@@ -54,35 +57,54 @@
 
 
 def kernel(
-    v, low_s, nb_own, omap_s, cnt_own, helm, t_fh, t_fl, t_bh, t_bl,
+    v, low_h, nb_own, omap_h, cnt_own, helm, table,
     out,
     vr, phys, hl, nl, upd, snd, ubuf, wsnd, rbuf, strs, zlow, onehot, oh, oht, hf, hth, htl,
-    fh, fl, bh, bl, nb_s, cnt_s, inv_s,
+    ft, bh, bl, nb_s, cnt_s, inv_s, low_s, omap_s,
     a_send, a_recv, i_send, i_recv, st_send, st_recv, b_send, b_recv, c_send, c_recv, l_sem,
 ):
     kx, ht, re = lax.axis_index("kx"), lax.axis_index("ht"), lax.axis_index("real")
+    kxs = [lax.rem(kx + d, NKX) for d in range(NKX)]
+    hts = [lax.rem(ht + d, NHT) for d in range(NHT)]
+
+    barrier = pltpu.get_barrier_semaphore()
+    for d in FAR_FIRST:
+        pl.semaphore_signal(barrier, 1, device_id=(kxs[d], ht, re), device_id_type=MESH)
+    for d in FAR_FIRST:
+        pl.semaphore_signal(barrier, 1, device_id=(kx, hts[d], re), device_id_type=MESH)
+    for d in (2, 1, 3):
+        pl.semaphore_signal(barrier, 1, device_id=(kx, ht, lax.rem(re + d, NREAL)), device_id_type=MESH)
     slot = kx * NHT + ht
     source = ht * NKX + kx
-    kxs = [lax.rem(kx + d, NKX) for d in range(NKX)]
-    hts = [lax.rem(ht + d, NHT) for d in range(NHT)]
-
-    barrier = pltpu.get_barrier_semaphore()
-    for d in range(1, NKX):
-        pl.semaphore_signal(barrier, 1, device_id=(lax.rem(kx + d, NKX), ht, re), device_id_type=MESH)
-    for d in range(1, NHT):
-        pl.semaphore_signal(barrier, 1, device_id=(kx, lax.rem(ht + d, NHT), re), device_id_type=MESH)
-    for d in range(1, NREAL):
-        pl.semaphore_signal(barrier, 1, device_id=(kx, ht, lax.rem(re + d, NREAL)), device_id_type=MESH)
-
+    pl.semaphore_wait(barrier, (NKX - 1) + (NHT - 1) + (NREAL - 1))
+
+    def gather(c):
+        for d in FAR_FIRST:
+            for a in range(2):
+                pltpu.make_async_remote_copy(
+                    v.at[c, 0, :, pl.ds(a * 32 + kxs[d] * 4, 4), :],
+                    vr.at[c, pl.ds(kx * BAND, BAND), pl.ds(a * 4, 4), :],
+                    a_send,
+                    a_recv.at[c],
+                    device_id=(kxs[d], ht, re),
+                    device_id_type=MESH,
+                ).start()
+
+    gather(ORDER[0])
+    for d in FAR_FIRST:
+        for own, held, i in ((nb_own, nb_s, 0), (cnt_own, cnt_s, 1)):
+            pltpu.make_async_remote_copy(
+                own, held.at[kx], i_send.at[i], i_recv.at[i], device_id=(kxs[d], ht, re), device_id_type=MESH
+            ).start()
+    for c in ORDER[1:]:
+        gather(c)
     local = [
         pltpu.make_async_copy(src, dst, l_sem.at[i])
-        for i, (src, dst) in enumerate(
-            ((helm.at[0], hf), (t_fh, fh), (t_fl, fl), (t_bh, bh), (t_bl, bl))
-        )
+        for i, (src, dst) in enumerate(((low_h, low_s), (omap_h, omap_s), (table, ft), (helm.at[0], hf)))
     ]
     for copy in local:
         copy.start()
-    for i, c in enumerate(ORDER):
+    for c in ORDER:
         for a in range(2):
             pltpu.make_async_copy(
                 v.at[c, 0, :, pl.ds(a * 32 + kx * 4, 4), :],
@@ -91,27 +113,8 @@
             ).start()
     pltpu.make_async_copy(nb_own, nb_s.at[kx], i_recv.at[0]).start()
     pltpu.make_async_copy(cnt_own, cnt_s.at[kx], i_recv.at[1]).start()
-
-    pl.semaphore_wait(barrier, (NKX - 1) + (NHT - 1) + (NREAL - 1))
-
-    for d in range(1, NKX):
-        peer = lax.rem(kx + d, NKX)
-        for own, table, i in ((nb_own, nb_s, 0), (cnt_own, cnt_s, 1)):
-            pltpu.make_async_remote_copy(
-                own, table.at[kx], i_send.at[i], i_recv.at[i], device_id=(peer, ht, re), device_id_type=MESH
-            ).start()
-    for c in ORDER:
-        for d in (4, 3, 5, 2, 6, 1, 7):
-            peer = lax.rem(kx + d, NKX)
-            for a in range(2):
-                pltpu.make_async_remote_copy(
-                    v.at[c, 0, :, pl.ds(a * 32 + peer * 4, 4), :],
-                    vr.at[c, pl.ds(kx * BAND, BAND), pl.ds(a * 4, 4), :],
-                    a_send.at[c],
-                    a_recv.at[c],
-                    device_id=(peer, ht, re),
-                    device_id_type=MESH,
-                ).start()
+    for copy in local:
+        copy.wait()
 
     lane = lax.broadcasted_iota(jnp.int32, (1, COLS), 1)
 
@@ -135,8 +138,8 @@
     lax.fori_loop(0, MODES, one_mode, 0)
     for c in range(COMP):
         zlow[c, LOW] = jnp.zeros((8, COLS), F32)
-    for copy in local:
-        copy.wait()
+    bh[...] = (ft[0].astype(F32).T * 0.5).astype(BF16)
+    bl[...] = (ft[1].astype(F32).T * 0.5).astype(BF16)
     for i in range(4):
         for j in range(4):
             block = hf[pl.ds(i * 128, 128), pl.ds(j * 128, 128)].T
@@ -149,27 +152,31 @@
     def products(c):
         pltpu.make_async_copy(vr.at[c], vr.at[c], a_recv.at[c]).wait()
         fields = vr[c].reshape(MODES * 8, COLS)
-        phys[c] = mm3(fields, fh[...], fl[...]).reshape(MODES, 8, POINTS)
-        def stress_band(band, sums):
-            sums = list(sums)
-            for row in range(BAND):
-                mine = phys[c, band * BAND + row] * (inv_s[band * BAND + row] == LOW).astype(F32)
-                for j in range(LOW):
-                    sums[j] = sums[j] + mine * phys[1, nb_s[band, row, j]]
-            return tuple(sums)
-
-        zeros = tuple(jnp.zeros((8, POINTS), F32) for _ in range(LOW))
-        stress = jnp.concatenate(lax.fori_loop(0, NKX, stress_band, zeros), axis=0)
-        strs[re, c] = mm3(stress * (1.0 / NREAL), bh[...], bl[...])
-        for d in range(1, NREAL):
-            pltpu.make_async_remote_copy(
-                strs.at[re, c],
-                strs.at[re, c],
-                st_send.at[c],
-                st_recv.at[c],
-                device_id=(kx, ht, lax.rem(re + d, NREAL)),
-                device_id_type=MESH,
-            ).start()
+        phys[c] = mm3(fields, ft[0], ft[1]).reshape(MODES, 8, POINTS)
+        for part in range(2):
+            members = range(part * 4, part * 4 + 4)
+
+            def stress_band(band, sums, members=members):
+                sums = list(sums)
+                for row in range(BAND):
+                    mine = phys[c, band * BAND + row] * (inv_s[band * BAND + row] == LOW).astype(F32)
+                    for i, j in enumerate(members):
+                        sums[i] = sums[i] + mine * phys[1, nb_s[band, row, j]]
+                return tuple(sums)
+
+            zeros = tuple(jnp.zeros((8, POINTS), F32) for _ in members)
+            stress = jnp.concatenate(lax.fori_loop(0, NKX, stress_band, zeros), axis=0)
+            here = strs.at[re, c, pl.ds(part * 32, 32)]
+            here[...] = mm3(stress * (1.0 / NREAL), bh[...], bl[...])
+            for d in (2, 1, 3):
+                pltpu.make_async_remote_copy(
+                    here,
+                    here,
+                    st_send,
+                    st_recv.at[c],
+                    device_id=(kx, ht, lax.rem(re + d, NREAL)),
+                    device_id_type=MESH,
+                ).start()
         low_1 = [phys[1, low_s[j]] for j in range(LOW)]
         low_c = low_1 if c == 1 else [phys[c, low_s[j]] for j in range(LOW)]
 
@@ -224,12 +231,12 @@
             snd.at[c, pl.ds(slot * 4, 4), :], ubuf.at[c, pl.ds(source * 4, 4), :], b_recv.at[c]
         ).start()
 
-        for t in range(1, SLOTS):
-            to_kx, to_ht = kxs[t % NKX], hts[t // NKX]
+        for dk, dh in PAIRS:
+            to_kx, to_ht = kxs[dk], hts[dh]
             pltpu.make_async_remote_copy(
                 snd.at[c, pl.ds((to_kx * NHT + to_ht) * 4, 4), :],
                 ubuf.at[c, pl.ds(source * 4, 4), :],
-                b_send.at[c],
+                b_send,
                 b_recv.at[c],
                 device_id=(to_kx, to_ht, re),
                 device_id_type=MESH,
@@ -259,12 +266,12 @@
             wsnd.at[c, pl.ds(ht * MODES + kx * 4, 4), :], rbuf.at[c, pl.ds(slot * 4, 4), :], c_recv.at[c]
         ).start()
 
-        for t in range(1, SLOTS):
-            to_kx, to_ht = kxs[t % NKX], hts[t // NKX]
+        for dk, dh in PAIRS:
+            to_kx, to_ht = kxs[dk], hts[dh]
             pltpu.make_async_remote_copy(
                 wsnd.at[c, pl.ds(to_ht * MODES + to_kx * 4, 4), :],
                 rbuf.at[c, pl.ds(slot * 4, 4), :],
-                c_send.at[c],
+                c_send,
                 c_recv.at[c],
                 device_id=(to_kx, to_ht, re),
                 device_id_type=MESH,
@@ -304,27 +311,24 @@
 
     pltpu.make_async_copy(nb_s.at[pl.ds(0, 7)], nb_s.at[pl.ds(0, 7)], i_send.at[0]).wait()
     pltpu.make_async_copy(cnt_s.at[pl.ds(0, 7)], cnt_s.at[pl.ds(0, 7)], i_send.at[1]).wait()
-    for c in range(COMP):
-        sent = vr.at[c, pl.ds(0, MODES - BAND)]
-        pltpu.make_async_copy(sent, sent, a_send.at[c]).wait()
-        sent = strs.at[pl.ds(0, NREAL - 1), c]
-        pltpu.make_async_copy(sent, sent, st_send.at[c]).wait()
-        sent = snd.at[c, pl.ds(0, 252), :]
-        pltpu.make_async_copy(sent, sent, b_send.at[c]).wait()
-        sent = wsnd.at[c, pl.ds(0, 252), :]
-        pltpu.make_async_copy(sent, sent, c_send.at[c]).wait()
+    for sent, sem in (
+        (vr.at[:, pl.ds(0, MODES - BAND)], a_send),
+        (strs.at[pl.ds(0, NREAL - 1)], st_send),
+        (snd.at[:, pl.ds(0, 252), :], b_send),
+        (wsnd.at[:, pl.ds(0, 252), :], c_send),
+    ):
+        pltpu.make_async_copy(sent, sent, sem).wait()
 
 
 def local(velocity, low_index, neighbours, owner_map, mode_counts, helmholtz):
-    tables = [jnp.asarray(t) for t in spanwise_tables()]
+    table = jnp.asarray(forward_table())
     hbm = pl.BlockSpec(memory_space=pl.ANY)
-    smem = pl.BlockSpec(memory_space=pltpu.SMEM)
     vmem = pl.BlockSpec(memory_space=pltpu.VMEM)
     dma = pltpu.SemaphoreType.DMA
     held = pl.pallas_call(
         kernel,
         out_shape=pltpu.VMEM(velocity.shape, F32),
-        in_specs=[hbm, smem, hbm, smem, hbm, hbm, hbm, hbm, hbm, hbm],
+        in_specs=[hbm] * 7,
         out_specs=vmem,
         scratch_shapes=[
             pltpu.VMEM((COMP, MODES, 8, COLS), F32),
@@ -344,27 +348,28 @@
             pltpu.VMEM((HEIGHTS, HEIGHTS), F32),
             pltpu.VMEM((HEIGHTS, HEIGHTS), BF16),
             pltpu.VMEM((HEIGHTS, HEIGHTS), BF16),
-            pltpu.VMEM((COLS, POINTS), BF16),
-            pltpu.VMEM((COLS, POINTS), BF16),
+            pltpu.VMEM((2, COLS, POINTS), BF16),
             pltpu.VMEM((POINTS, COLS), BF16),
             pltpu.VMEM((POINTS, COLS), BF16),
             pltpu.SMEM((NKX, BAND, LOW), jnp.int32),
             pltpu.SMEM((NKX, BAND), jnp.int32),
             pltpu.SMEM((MODES,), jnp.int32),
-            dma((COMP,)),
+            pltpu.SMEM((LOW,), jnp.int32),
+            pltpu.SMEM((SLOTS,), jnp.int32),
+            dma,
             dma((COMP,)),
             dma((2,)),
             dma((2,)),
+            dma,
             dma((COMP,)),
+            dma,
             dma((COMP,)),
+            dma,
             dma((COMP,)),
-            dma((COMP,)),
-            dma((COMP,)),
-            dma((COMP,)),
-            dma((5,)),
+            dma((4,)),
         ],
         compiler_params=pltpu.CompilerParams(collective_id=0, has_side_effects=True),
-    )(velocity, low_index, neighbours, owner_map, mode_counts, helmholtz, *tables)
+    )(velocity, low_index, neighbours, owner_map, mode_counts, helmholtz, table)
     return held
 
 

time: 46.1 us -> 44.3 us (0.961)
  Pallas kernels: 45.2 us -> 43.5 us
    pallas_call x1, Pallas kernels: 45.2 us -> 43.5 us  [local(): pl.pallas_call(kernel, out_shape=pltpu.VMEM(velocity.shape, F32), in_spec...]
where the time goes in v3:
time: 44.3 us; the launch traced here: 44.2 us
  Pallas kernels  43.5 us (98%)
  local copies, waits for them, and re-layouts  0.75 us (2%)
    pallas_call x1, Pallas kernels, local(): pl.pallas_call(kernel, out_shape=pltpu.VMEM(velocity.shape, F32), in_spec...  43.5 us

profile of v3, /device:TPU:1, one launch (start us, length us, event | category | flops | bytes accessed | tf_op | source)
XLA Modules:
  0.0 44.2 jit_solution(3386867436732670449)
XLA Ops:
  0.0 43.5 %shard_map.73 = f32[3,1,4,64,128]{4,3,2,1,0:T(8,128)S(1)} custom-call(f32[3,1,4,64,128]{4,3,2,1,0:T(8,128)} %v.1, s32[8]{0:T(128)} %low_h.1, s32[4,8]{1,0:T(4,128)} %nb_own.1, s32[64]{0:T(128)} %omap_h.1, s32[4]{0:T(128)} %cnt_own.1, f32[1,512,512]{2,1,0:T(8,128)} %helm.1, bf16[2,128,256]{2,1,0:T(8,128)(2,1)} %constant.2.clone.table), custom_call_target="tpu_custom_call" | custom-call | tf_op jit(solution)/shard_map/pallas_call | solution.py:328
  43.5 0.7 %copy.9 = f32[3,1,4,64,128]{4,3,2,1,0:T(8,128)} copy(f32[3,1,4,64,128]{4,3,2,1,0:T(8,128)S(1)} %shard_map.73) | data formatting | bytes 786432

commit v4 on v3

v4 whole, which is shorter than its diff:
```python
import functools

import jax
import jax.numpy as jnp
import numpy as np
from jax import lax
from jax.experimental import pallas as pl
from jax.experimental.pallas import tpu as pltpu
from jax.sharding import PartitionSpec as P

MESH = pl.DeviceIdType.MESH
F32 = jnp.float32
BF16 = jnp.bfloat16

dt_step = 0.1


def ring(step, count):
    return min(step, count - step)


COMP, BAND, ROWS, COLS = 3, 4, 64, 128
NKX, NHT, NREAL = 8, 8, 4
MODES, LOW, POINTS, HEIGHTS, SLOTS = 32, 8, 256, 512, 64
HIGH = MODES - LOW
ORDER = (1, 0, 2)
FAR_FIRST = (4, 3, 5, 2, 6, 1, 7)
PAIRS = [(dk, dh) for dk in range(NKX) for dh in range(NHT) if dk + dh]
PAIRS.sort(key=lambda p: (-ring(p[1] // 2, NHT // 2), -ring(p[0], NKX)))


def forward_table():
    ids = np.arange(COLS)
    wave = (ids // 2).astype(np.float32)
    spots = np.float32(2.0 * np.pi) * np.arange(POINTS).astype(np.float32) / np.float32(POINTS)
    phases = (wave[:, None] * spots[None, :]).astype(np.float64)
    forward = (np.where(ids[:, None] % 2 == 0, np.cos(phases), -np.sin(phases)) / 8.0).astype(np.float32)
    head = forward.astype(BF16)
    return np.stack([head, head, (forward - head.astype(np.float32)).astype(BF16)])


def split(x):
    head = x.astype(BF16)
    return head, (x - head.astype(F32)).astype(BF16)


def mm(a, b):
    return lax.dot_general(a, b, (((1,), (0,)), ((), ())), preferred_element_type=F32)


def mm_nt(a, b):
    return lax.dot_general(a, b, (((1,), (1,)), ((), ())), preferred_element_type=F32)


def apply_forward(x, table):
    hi, lo = split(x)
    heads = table[pl.ds(0, 2)].reshape(2 * COLS, POINTS)
    return mm(jnp.concatenate([hi, lo], axis=1), heads) + mm(hi, table[2])


def apply_backward(x, both):
    hi, lo = split(x)
    part = mm(hi, both[...])
    return part[:, :COLS] + (part[:, COLS:] + mm(lo, both[:, :COLS]))


def kernel(
    v, low_h, nb_own, omap_h, cnt_own, helm, table,
    out,
    vr, cur, phys, hl, nl, upd, snd, ubuf, lsnd, lbuf, wsnd, rbuf, strs, onehot, oh, oht, order, om, hf, ht32, hth, htl,
    ft, back_t, nb_s, cnt_b, cnt_s, perm_s, low_s, omap_s,
    a_send, a_recv, i_send, i_recv, st_send, st_recv, h_send, h_recv, b_send, b_recv, c_send, c_recv, l_sem,
):
    kx, ht, re = lax.axis_index("kx"), lax.axis_index("ht"), lax.axis_index("real")
    kxs = [lax.rem(kx + d, NKX) for d in range(NKX)]
    hts = [lax.rem(ht + d, NHT) for d in range(NHT)]

    barrier = pltpu.get_barrier_semaphore()
    for d in FAR_FIRST:
        pl.semaphore_signal(barrier, 1, device_id=(kxs[d], ht, re), device_id_type=MESH)
    for d in FAR_FIRST:
        pl.semaphore_signal(barrier, 1, device_id=(kx, hts[d], re), device_id_type=MESH)
    for d in (2, 1, 3):
        pl.semaphore_signal(barrier, 1, device_id=(kx, ht, lax.rem(re + d, NREAL)), device_id_type=MESH)
    slot = kx * NHT + ht
    source = ht * NKX + kx
    pl.semaphore_wait(barrier, (NKX - 1) + (NHT - 1) + (NREAL - 1))

    def gather(c):
        for d in FAR_FIRST:
            pltpu.make_async_remote_copy(
                v.at[c, 0, :, pl.ds(kxs[d] * 8, 8), :],
                vr.at[c, pl.ds(kx * BAND, BAND)],
                a_send,
                a_recv.at[c],
                device_id=(kxs[d], ht, re),
                device_id_type=MESH,
            ).start()

    gather(ORDER[0])
    for d in FAR_FIRST:
        for own, held, i in ((nb_own, nb_s.at[pl.ds(kx * BAND, BAND)], 0), (cnt_own, cnt_b.at[kx], 1)):
            pltpu.make_async_remote_copy(
                own, held, i_send.at[i], i_recv.at[i], device_id=(kxs[d], ht, re), device_id_type=MESH
            ).start()
    for c in ORDER[1:]:
        gather(c)
    local = [
        pltpu.make_async_copy(src, dst, l_sem.at[i])
        for i, (src, dst) in enumerate(((low_h, low_s), (omap_h, omap_s), (table, ft), (helm.at[0], hf)))
    ]
    for copy in local:
        copy.start()
    for c in ORDER:
        pltpu.make_async_copy(
            v.at[c, 0, :, pl.ds(kx * 8, 8), :], vr.at[c, pl.ds(kx * BAND, BAND)], a_recv.at[c]
        ).start()
    pltpu.make_async_copy(nb_own, nb_s.at[pl.ds(kx * BAND, BAND)], i_recv.at[0]).start()
    pltpu.make_async_copy(cnt_own, cnt_b.at[kx], i_recv.at[1]).start()
    for copy in local:
        copy.wait()

    lane = lax.broadcasted_iota(jnp.int32, (1, COLS), 1)

    def one_row(s, _):
        for p in range(2):
            onehot[pl.ds(p * SLOTS + s, 1), :] = (lane == 2 * omap_s[s] + p).astype(F32)
        return 0

    lax.fori_loop(0, SLOTS, one_row, 0)
    square = onehot[...]
    turn = square.T
    for i in range(2):
        oh[:, pl.ds(i * 128, 128)] = square.astype(BF16)
        oht[:, pl.ds(i * 128, 128)] = turn.astype(BF16)

    lows = [low_s[j] for j in range(LOW)]
    ranked = list(lows)
    for i in range(LOW):
        for j in range(i % 2, LOW - 1, 2):
            one, two = ranked[j], ranked[j + 1]
            ranked[j], ranked[j + 1] = jnp.minimum(one, two), jnp.maximum(one, two)

    def one_high(q, _):
        mode = q
        for low in ranked:
            mode = mode + (low <= mode).astype(jnp.int32)
        perm_s[q] = mode
        return 0

    lax.fori_loop(0, HIGH, one_high, 0)
    for j in range(LOW):
        perm_s[HIGH + j] = lows[j]

    def one_mode(m, _):
        place = m
        for low in lows:
            place = place - (low < m).astype(jnp.int32)
        for j, low in enumerate(lows):
            place = jnp.where(low == m, jnp.int32(HIGH + j), place)
        order[pl.ds(m, 1), :] = (lane == place).astype(F32)
        order[pl.ds(MODES + m, 1), :] = (lane == MODES + place).astype(F32)
        return 0

    lax.fori_loop(0, MODES, one_mode, 0)
    om[...] = order[:, : 2 * MODES].astype(BF16)
    back_t[:, pl.ds(0, COLS)] = (ft[0].astype(F32).T * 0.5).astype(BF16)
    back_t[:, pl.ds(COLS, COLS)] = (ft[2].astype(F32).T * 0.5).astype(BF16)
    for i in range(4):
        for j in range(4):
            ht32[i, pl.ds(j * 128, 128), :] = hf[pl.ds(i * 128, 128), pl.ds(j * 128, 128)].T
    for y in range(4):
        for a in range(2):
            for i in range(4):
                rows = [ht32[i, pl.ds(h * 64 + a * 4 + y, NKX, stride=8), :] for h in range(NHT)]
                head, tail = split(jnp.concatenate(rows, axis=0))
                hth[pl.ds((y * 2 + a) * 64, 64), pl.ds(i * 128, 128)] = head
                htl[pl.ds((y * 2 + a) * 64, 64), pl.ds(i * 128, 128)] = tail
    pltpu.make_async_copy(nb_s, nb_s, i_recv.at[0]).wait()
    pltpu.make_async_copy(cnt_b, cnt_b, i_recv.at[1]).wait()
    for m in range(MODES):
        cnt_s[m] = cnt_b[m // BAND, m % BAND]

    def products(c):
        pltpu.make_async_copy(vr.at[c], vr.at[c], a_recv.at[c]).wait()
        fields = vr[c].reshape(MODES * 8, COLS)
        cur[c] = vr[c]
        phys[c] = apply_forward(fields, ft).reshape(MODES, 8, POINTS)
        for part in range(2):
            members = range(part * 4, part * 4 + 4)

            def stress_band(band, sums, members=members):
                sums = list(sums)
                for row in range(BAND):
                    mode = perm_s[band * BAND + row]
                    mine = phys[c, mode]
                    for i, j in enumerate(members):
                        sums[i] = sums[i] + mine * phys[1, nb_s[mode, j]]
                return tuple(sums)

            zeros = tuple(jnp.zeros((8, POINTS), F32) for _ in members)
            stress = jnp.concatenate(lax.fori_loop(0, HIGH // BAND, stress_band, zeros), axis=0)
            here = strs.at[re, c, pl.ds(part * 32, 32)]
            here[...] = apply_backward(stress * (1.0 / NREAL), back_t)
            for d in (2, 1, 3):
                pltpu.make_async_remote_copy(
                    here,
                    here,
                    st_send,
                    st_recv.at[c],
                    device_id=(kx, ht, lax.rem(re + d, NREAL)),
                    device_id_type=MESH,
                ).start()
        low_1 = [phys[1, low_s[j]] for j in range(LOW)]
        low_c = low_1 if c == 1 else [phys[c, low_s[j]] for j in range(LOW)]

        def high_band(band, _):
            for row in range(BAND):
                mode = perm_s[band * BAND + row]
                first, second = [], []
                for j in range(LOW):
                    near = nb_s[mode, j]
                    first.append(low_c[j] * phys[1, near])
                    if c != 1:
                        second.append(low_1[j] * phys[c, near])
                total = functools.reduce(lambda a, b: a + b, first)
                total = total + (total if c == 1 else functools.reduce(lambda a, b: a + b, second))
                hl[band * BAND + row] = total
            return 0

        lax.fori_loop(0, HIGH // BAND, high_band, 0)
        nl[c] = apply_backward(hl[...].reshape(HIGH * 8, POINTS), back_t).reshape(HIGH, 8, COLS)

    half_lane = lax.broadcasted_iota(jnp.int32, (8, COLS), 1) // 2
    odd = (lax.broadcasted_iota(jnp.int32, (SLOTS, 128), 1) // 32) % 2 == 1

    def gain(mode):
        return jnp.where(half_lane < cnt_s[mode], F32(dt_step), F32(0.0))

    def turned(tiles):
        rows = [
            upd[pl.ds(group * 64 + a * 4 + y, 8, stride=8), :]
            for pair in tiles
            for a in range(2)
            for group in pair
            for y in range(4)
        ]
        hi, lo = split(jnp.concatenate(rows, axis=0))
        both = mm_nt(oh[...], jnp.concatenate([hi, lo], axis=1))
        given = []
        for tile in range(len(tiles)):
            even_p = both[:SLOTS, tile * 128 : tile * 128 + 128]
            odd_p = both[SLOTS:, tile * 128 : tile * 128 + 128]
            given.append(jnp.where(odd, pltpu.roll(odd_p, 32, 1), even_p))
            given.append(jnp.where(odd, odd_p, pltpu.roll(even_p, 96, 1)))
        return given

    def to_owners(given, taken, stride, count, send, recv):
        pltpu.make_async_copy(
            given.at[pl.ds(slot * stride, count), :], taken.at[pl.ds(source * stride, count), :], recv
        ).start()
        for dk, dh in PAIRS:
            to_kx, to_ht = kxs[dk], hts[dh]
            pltpu.make_async_remote_copy(
                given.at[pl.ds((to_kx * NHT + to_ht) * stride, count), :],
                taken.at[pl.ds(source * stride, count), :],
                send,
                recv,
                device_id=(to_kx, to_ht, re),
                device_id_type=MESH,
            ).start()

    def forced_high(c):
        def one_band(band, _):
            for row in range(BAND):
                q = band * BAND + row
                mode = perm_s[q]
                upd[pl.ds(q * 8, 8), :] = cur[c, mode] + gain(mode) * nl[c, q]
            return 0

        lax.fori_loop(0, HIGH // BAND, one_band, 0)
        for group, value in enumerate(turned(((0, 1), (2, 2)))[:3]):
            snd[c, pl.ds(group, SLOTS, stride=4), :] = value

    def forced_low(c):
        pltpu.make_async_copy(strs.at[pl.ds(0, 3), 0], strs.at[pl.ds(0, 3), 0], st_recv.at[c]).wait()
        summed = (strs[0, c] + strs[1, c]) + (strs[2, c] + strs[3, c])
        for j in range(LOW):
            mode = low_s[j]
            upd[pl.ds((HIGH + j) * 8, 8), :] = cur[c, mode] + gain(mode) * summed[j * 8 : j * 8 + 8]
        value = turned(((3, 3),))[0]
        if c == ORDER[2]:
            lsnd[...] = value
        else:
            snd[ORDER[ORDER.index(c) + 1], pl.ds(3, SLOTS, stride=4), :] = value

    first_half = lax.broadcasted_iota(jnp.int32, (MODES, 128), 1) < 64

    def solved(c):
        place = ORDER.index(c)
        if place == 0:
            arrived = ubuf.at[c, pl.ds(0, 3 * SLOTS), :]
            pltpu.make_async_copy(arrived, arrived, h_recv.at[c]).wait()
        if place < 2:
            arrived = ubuf.at[ORDER[place + 1]]
            pltpu.make_async_copy(arrived, arrived, h_recv.at[ORDER[place + 1]]).wait()
        else:
            pltpu.make_async_copy(lbuf, lbuf, b_recv).wait()
        groups = []
        for group in range(4):
            if group < 3:
                given = ubuf[c, pl.ds(group, SLOTS, stride=4), :]
            else:
                given = lbuf[...] if place == 2 else ubuf[ORDER[place + 1], pl.ds(3, SLOTS, stride=4), :]
            groups.append(jnp.concatenate([given, pltpu.roll(given, 64, 1)], axis=0).T[:64])
        fields = jnp.concatenate(
            [
                jnp.concatenate([groups[g][(p * 4 + y) * 8 : (p * 4 + y) * 8 + 8] for y in range(4)], axis=1)
                for p in range(2)
                for g in range(4)
            ],
            axis=0,
        )
        hi, lo = split(fields)
        hi = mm(om[...], hi).astype(BF16)
        lo = mm(om[...], lo).astype(BF16)
        part = mm(jnp.concatenate([hi, lo], axis=0), hth[...])
        answer = part[: 2 * MODES] + (mm(hi, htl[...]) + part[2 * MODES :])
        for tile in range(4):
            even_p = answer[:MODES, tile * 128 : tile * 128 + 128]
            odd_p = answer[MODES:, tile * 128 : tile * 128 + 128]
            wsnd[c, pl.ds((2 * tile) * MODES, MODES), :] = jnp.where(
                first_half, even_p, pltpu.roll(odd_p, 64, 1)
            )
            wsnd[c, pl.ds((2 * tile + 1) * MODES, MODES), :] = jnp.where(
                first_half, pltpu.roll(even_p, 64, 1), odd_p
            )
        pltpu.make_async_copy(
            wsnd.at[c, pl.ds(ht * MODES + kx * 4, 4), :], rbuf.at[c, pl.ds(slot * 4, 4), :], c_recv.at[c]
        ).start()

        for dk, dh in PAIRS:
            to_kx, to_ht = kxs[dk], hts[dh]
            pltpu.make_async_remote_copy(
                wsnd.at[c, pl.ds(to_ht * MODES + to_kx * 4, 4), :],
                rbuf.at[c, pl.ds(slot * 4, 4), :],
                c_send,
                c_recv.at[c],
                device_id=(to_kx, to_ht, re),
                device_id_type=MESH,
            ).start()

    def placed(c):
        pltpu.make_async_copy(rbuf.at[c], rbuf.at[c], c_recv.at[c]).wait()
        low_half = lax.broadcasted_iota(jnp.int32, (SLOTS, 128), 1) < 64
        columns = []
        for pair in range(2):
            one = rbuf[c, pl.ds(2 * pair, SLOTS, stride=4), :]
            two = rbuf[c, pl.ds(2 * pair + 1, SLOTS, stride=4), :]
            columns.append(
                jnp.concatenate(
                    [
                        jnp.where(low_half, one, pltpu.roll(two, 64, 1)),
                        jnp.where(low_half, pltpu.roll(one, 64, 1), two),
                    ],
                    axis=0,
                )
            )
        hi, lo = split(jnp.concatenate(columns, axis=1))
        back = mm(oht[...], jnp.concatenate([hi, lo], axis=0))
        for pair in range(2):
            out[c, 0, pl.ds(2 * pair, 2), :, :] = back[:, pair * 128 : pair * 128 + 128].T.reshape(2, ROWS, COLS)

    one, two, three = ORDER
    products(one)
    forced_high(one)
    to_owners(snd.at[one], ubuf.at[one], 4, 3, h_send, h_recv.at[one])
    products(two)
    forced_high(two)
    forced_low(one)
    to_owners(snd.at[two], ubuf.at[two], 4, 4, h_send, h_recv.at[two])
    products(three)
    forced_high(three)
    forced_low(two)
    to_owners(snd.at[three], ubuf.at[three], 4, 4, h_send, h_recv.at[three])
    forced_low(three)
    to_owners(lsnd, lbuf, 1, 1, b_send, b_recv)
    for c in ORDER:
        solved(c)
    for c in ORDER:
        placed(c)

    pltpu.make_async_copy(nb_s.at[pl.ds(0, 28)], nb_s.at[pl.ds(0, 28)], i_send.at[0]).wait()
    pltpu.make_async_copy(cnt_b.at[pl.ds(0, 7)], cnt_b.at[pl.ds(0, 7)], i_send.at[1]).wait()
    for sent, sem in (
        (vr.at[:, pl.ds(0, MODES - BAND)], a_send),
        (strs.at[pl.ds(0, NREAL - 1)], st_send),
        (snd.at[:, pl.ds(0, 231), :], h_send),
        (lsnd.at[pl.ds(0, 63), :], b_send),
        (wsnd.at[:, pl.ds(0, 252), :], c_send),
    ):
        pltpu.make_async_copy(sent, sent, sem).wait()


def local(velocity, low_index, neighbours, owner_map, mode_counts, helmholtz):
    table = jnp.asarray(forward_table())
    hbm = pl.BlockSpec(memory_space=pl.ANY)
    vmem = pl.BlockSpec(memory_space=pltpu.VMEM)
    dma = pltpu.SemaphoreType.DMA
    held = pl.pallas_call(
        kernel,
        out_shape=pltpu.VMEM(velocity.shape, F32),
        in_specs=[hbm] * 7,
        out_specs=vmem,
        scratch_shapes=[
            pltpu.VMEM((COMP, MODES, 8, COLS), F32),
            pltpu.VMEM((COMP, MODES, 8, COLS), F32),
            pltpu.VMEM((COMP, MODES, 8, POINTS), F32),
            pltpu.VMEM((HIGH, 8, POINTS), F32),
            pltpu.VMEM((COMP, HIGH, 8, COLS), F32),
            pltpu.VMEM((MODES * 8, COLS), F32),
            pltpu.VMEM((COMP, 256, 128), F32),
            pltpu.VMEM((COMP, 256, 128), F32),
            pltpu.VMEM((SLOTS, 128), F32),
            pltpu.VMEM((SLOTS, 128), F32),
            pltpu.VMEM((COMP, 256, 128), F32),
            pltpu.VMEM((COMP, 256, 128), F32),
            pltpu.VMEM((NREAL, COMP, LOW * 8, COLS), F32),
            pltpu.VMEM((128, COLS), F32),
            pltpu.VMEM((128, 2 * COLS), BF16),
            pltpu.VMEM((COLS, 256), BF16),
            pltpu.VMEM((2 * MODES, 128), F32),
            pltpu.VMEM((2 * MODES, 2 * MODES), BF16),
            pltpu.VMEM((HEIGHTS, HEIGHTS), F32),
            pltpu.VMEM((4, HEIGHTS, 128), F32),
            pltpu.VMEM((HEIGHTS, HEIGHTS), BF16),
            pltpu.VMEM((HEIGHTS, HEIGHTS), BF16),
            pltpu.VMEM((3, COLS, POINTS), BF16),
            pltpu.VMEM((POINTS, 2 * COLS), BF16),
            pltpu.SMEM((MODES, LOW), jnp.int32),
            pltpu.SMEM((NKX, BAND), jnp.int32),
            pltpu.SMEM((MODES,), jnp.int32),
            pltpu.SMEM((MODES,), jnp.int32),
            pltpu.SMEM((LOW,), jnp.int32),
            pltpu.SMEM((SLOTS,), jnp.int32),
            dma,
            dma((COMP,)),
            dma((2,)),
            dma((2,)),
            dma,
            dma((COMP,)),
            dma,
            dma((COMP,)),
            dma,
            dma,
            dma,
            dma((COMP,)),
            dma((4,)),
        ],
        compiler_params=pltpu.CompilerParams(collective_id=0, has_side_effects=True),
    )(velocity, low_index, neighbours, owner_map, mode_counts, helmholtz, table)
    return held


def solution(mesh):
    in_specs = (
        P(None, "real", "kx", "ht", None),
        P(),
        P("kx", None),
        P(),
        P("kx"),
        P(("kx", "ht"), None, None),
    )
    out_specs = P(None, "real", "kx", "ht", None)
    return jax.shard_map(local, mesh=mesh, in_specs=in_specs, out_specs=out_specs, check_vma=False)
```

time: 44.3 us -> 43.4 us (0.980)
  Pallas kernels: 43.5 us -> 42.6 us
    pallas_call x1, Pallas kernels: 43.5 us -> 42.6 us  [local(): pl.pallas_call(kernel, out_shape=pltpu.VMEM(velocity.shape, F32), in_spec...]
where the time goes in v4:
time: 43.4 us
  Pallas kernels  42.6 us (98%)
  local copies, waits for them, and re-layouts  0.75 us (2%)
    pallas_call x1, Pallas kernels, local(): pl.pallas_call(kernel, out_shape=pltpu.VMEM(velocity.shape, F32), in_spec...  42.6 us

profile of v4, /device:TPU:1, one launch (start us, length us, event | category | flops | bytes accessed | tf_op | source)
XLA Modules:
  0.0 43.4 jit_solution(7804002544214264505)
XLA Ops:
  0.0 42.6 %shard_map.73 = f32[3,1,4,64,128]{4,3,2,1,0:T(8,128)S(1)} custom-call(f32[3,1,4,64,128]{4,3,2,1,0:T(8,128)} %v.1, s32[8]{0:T(128)} %low_h.1, s32[4,8]{1,0:T(4,128)} %nb_own.1, s32[64]{0:T(128)} %omap_h.1, s32[4]{0:T(128)} %cnt_own.1, f32[1,512,512]{2,1,0:T(8,128)} %helm.1, bf16[3,128,256]{2,1,0:T(8,128)(2,1)} %constant.2.clone.table), custom_call_target="tpu_custom_call" | custom-call | tf_op jit(solution)/shard_map/pallas_call | solution.py:410
  42.6 0.7 %copy.9 = f32[3,1,4,64,128]{4,3,2,1,0:T(8,128)} copy(f32[3,1,4,64,128]{4,3,2,1,0:T(8,128)S(1)} %shard_map.73) | data formatting | bytes 786432

commit v5 on v4

--- a/solution.py
+++ b/solution.py
@@ -67,7 +67,7 @@
 def kernel(
     v, low_h, nb_own, omap_h, cnt_own, helm, table,
     out,
-    vr, cur, phys, hl, nl, upd, snd, ubuf, lsnd, lbuf, wsnd, rbuf, strs, onehot, oh, oht, order, om, hf, ht32, hth, htl,
+    vr, cur, phys, hl, nl, upd, snd, ubuf, lsnd, lbuf, fsnd, fbuf, wsnd, rbuf, strs, onehot, oh, oht, order, om, hf, ht32, hth, htl,
     ft, back_t, nb_s, cnt_b, cnt_s, perm_s, low_s, omap_s,
     a_send, a_recv, i_send, i_recv, st_send, st_recv, h_send, h_recv, b_send, b_recv, c_send, c_recv, l_sem,
 ):
@@ -186,31 +186,28 @@
         fields = vr[c].reshape(MODES * 8, COLS)
         cur[c] = vr[c]
         phys[c] = apply_forward(fields, ft).reshape(MODES, 8, POINTS)
-        for part in range(2):
-            members = range(part * 4, part * 4 + 4)
-
-            def stress_band(band, sums, members=members):
-                sums = list(sums)
-                for row in range(BAND):
-                    mode = perm_s[band * BAND + row]
-                    mine = phys[c, mode]
-                    for i, j in enumerate(members):
-                        sums[i] = sums[i] + mine * phys[1, nb_s[mode, j]]
-                return tuple(sums)
-
-            zeros = tuple(jnp.zeros((8, POINTS), F32) for _ in members)
-            stress = jnp.concatenate(lax.fori_loop(0, HIGH // BAND, stress_band, zeros), axis=0)
-            here = strs.at[re, c, pl.ds(part * 32, 32)]
-            here[...] = apply_backward(stress * (1.0 / NREAL), back_t)
-            for d in (2, 1, 3):
-                pltpu.make_async_remote_copy(
-                    here,
-                    here,
-                    st_send,
-                    st_recv.at[c],
-                    device_id=(kx, ht, lax.rem(re + d, NREAL)),
-                    device_id_type=MESH,
-                ).start()
+        def stress_band(band, sums):
+            sums = list(sums)
+            for row in range(BAND):
+                mode = perm_s[band * BAND + row]
+                mine = phys[c, mode]
+                for j in range(LOW):
+                    sums[j] = sums[j] + mine * phys[1, nb_s[mode, j]]
+            return tuple(sums)
+
+        zeros = tuple(jnp.zeros((8, POINTS), F32) for _ in range(LOW))
+        stress = jnp.concatenate(lax.fori_loop(0, HIGH // BAND, stress_band, zeros), axis=0)
+        here = strs.at[re, c]
+        here[...] = apply_backward(stress * (1.0 / NREAL), back_t)
+        for d in (2, 1, 3):
+            pltpu.make_async_remote_copy(
+                here,
+                here,
+                st_send,
+                st_recv.at[c],
+                device_id=(kx, ht, lax.rem(re + d, NREAL)),
+                device_id_type=MESH,
+            ).start()
         low_1 = [phys[1, low_s[j]] for j in range(LOW)]
         low_c = low_1 if c == 1 else [phys[c, low_s[j]] for j in range(LOW)]
 
@@ -291,6 +288,8 @@
         value = turned(((3, 3),))[0]
         if c == ORDER[2]:
             lsnd[...] = value
+        elif c == ORDER[0]:
+            fsnd[...] = value
         else:
             snd[ORDER[ORDER.index(c) + 1], pl.ds(3, SLOTS, stride=4), :] = value
 
@@ -301,17 +300,20 @@
         if place == 0:
             arrived = ubuf.at[c, pl.ds(0, 3 * SLOTS), :]
             pltpu.make_async_copy(arrived, arrived, h_recv.at[c]).wait()
-        if place < 2:
-            arrived = ubuf.at[ORDER[place + 1]]
-            pltpu.make_async_copy(arrived, arrived, h_recv.at[ORDER[place + 1]]).wait()
+            pltpu.make_async_copy(fbuf, fbuf, b_recv.at[0]).wait()
+        elif place == 1:
+            arrived = ubuf.at[c, pl.ds(0, 3 * SLOTS), :]
+            pltpu.make_async_copy(arrived, arrived, h_recv.at[c]).wait()
+            pltpu.make_async_copy(ubuf.at[ORDER[2]], ubuf.at[ORDER[2]], h_recv.at[ORDER[2]]).wait()
         else:
-            pltpu.make_async_copy(lbuf, lbuf, b_recv).wait()
+            pltpu.make_async_copy(lbuf, lbuf, b_recv.at[1]).wait()
         groups = []
         for group in range(4):
             if group < 3:
                 given = ubuf[c, pl.ds(group, SLOTS, stride=4), :]
             else:
-                given = lbuf[...] if place == 2 else ubuf[ORDER[place + 1], pl.ds(3, SLOTS, stride=4), :]
+                low = (fbuf, None, lbuf)[place]
+                given = ubuf[ORDER[2], pl.ds(3, SLOTS, stride=4), :] if place == 1 else low[...]
             groups.append(jnp.concatenate([given, pltpu.roll(given, 64, 1)], axis=0).T[:64])
         fields = jnp.concatenate(
             [
@@ -377,14 +379,15 @@
     to_owners(snd.at[one], ubuf.at[one], 4, 3, h_send, h_recv.at[one])
     products(two)
     forced_high(two)
+    to_owners(snd.at[two], ubuf.at[two], 4, 3, h_send, h_recv.at[two])
     forced_low(one)
-    to_owners(snd.at[two], ubuf.at[two], 4, 4, h_send, h_recv.at[two])
+    to_owners(fsnd, fbuf, 1, 1, b_send.at[0], b_recv.at[0])
     products(three)
     forced_high(three)
     forced_low(two)
     to_owners(snd.at[three], ubuf.at[three], 4, 4, h_send, h_recv.at[three])
     forced_low(three)
-    to_owners(lsnd, lbuf, 1, 1, b_send, b_recv)
+    to_owners(lsnd, lbuf, 1, 1, b_send.at[1], b_recv.at[1])
     for c in ORDER:
         solved(c)
     for c in ORDER:
@@ -395,8 +398,9 @@
     for sent, sem in (
         (vr.at[:, pl.ds(0, MODES - BAND)], a_send),
         (strs.at[pl.ds(0, NREAL - 1)], st_send),
-        (snd.at[:, pl.ds(0, 231), :], h_send),
-        (lsnd.at[pl.ds(0, 63), :], b_send),
+        (snd.at[:, pl.ds(0, 210), :], h_send),
+        (fsnd.at[pl.ds(0, 63), :], b_send.at[0]),
+        (lsnd.at[pl.ds(0, 63), :], b_send.at[1]),
         (wsnd.at[:, pl.ds(0, 252), :], c_send),
     ):
         pltpu.make_async_copy(sent, sent, sem).wait()
@@ -421,6 +425,8 @@
             pltpu.VMEM((MODES * 8, COLS), F32),
             pltpu.VMEM((COMP, 256, 128), F32),
             pltpu.VMEM((COMP, 256, 128), F32),
+            pltpu.VMEM((SLOTS, 128), F32),
+            pltpu.VMEM((SLOTS, 128), F32),
             pltpu.VMEM((SLOTS, 128), F32),
             pltpu.VMEM((SLOTS, 128), F32),
             pltpu.VMEM((COMP, 256, 128), F32),
@@ -451,8 +457,8 @@
             dma((COMP,)),
             dma,
             dma((COMP,)),
-            dma,
-            dma,
+            dma((2,)),
+            dma((2,)),
             dma,
             dma((COMP,)),
             dma((4,)),

time: 43.4 us -> 43 us (level)
    pallas_call x1, Pallas kernels: 42.6 us -> 42.2 us  [local(): pl.pallas_call(kernel, out_shape=pltpu.VMEM(velocity.shape, F32), in_spec...]
where the time goes in v5:
time: 43 us; the launch traced here: 42.9 us
  Pallas kernels  42.2 us (98%)
  local copies, waits for them, and re-layouts  0.75 us (2%)
    pallas_call x1, Pallas kernels, local(): pl.pallas_call(kernel, out_shape=pltpu.VMEM(velocity.shape, F32), in_spec...  42.2 us

profile of v5, /device:TPU:1, one launch (start us, length us, event | category | flops | bytes accessed | tf_op | source)
XLA Modules:
  0.0 42.9 jit_solution(14480472004919018713)
XLA Ops:
  0.0 42.2 %shard_map.73 = f32[3,1,4,64,128]{4,3,2,1,0:T(8,128)S(1)} custom-call(f32[3,1,4,64,128]{4,3,2,1,0:T(8,128)} %v.1, s32[8]{0:T(128)} %low_h.1, s32[4,8]{1,0:T(4,128)} %nb_own.1, s32[64]{0:T(128)} %omap_h.1, s32[4]{0:T(128)} %cnt_own.1, f32[1,512,512]{2,1,0:T(8,128)} %helm.1, bf16[3,128,256]{2,1,0:T(8,128)(2,1)} %constant.2.clone.table), custom_call_target="tpu_custom_call" | custom-call | tf_op jit(solution)/shard_map/pallas_call | solution.py:414
  42.2 0.7 %copy.9 = f32[3,1,4,64,128]{4,3,2,1,0:T(8,128)} copy(f32[3,1,4,64,128]{4,3,2,1,0:T(8,128)S(1)} %shard_map.73) | data formatting | bytes 786432

commit v6 on v5

--- a/solution.py
+++ b/solution.py
@@ -97,12 +97,12 @@
                 device_id_type=MESH,
             ).start()
 
-    gather(ORDER[0])
     for d in FAR_FIRST:
         for own, held, i in ((nb_own, nb_s.at[pl.ds(kx * BAND, BAND)], 0), (cnt_own, cnt_b.at[kx], 1)):
             pltpu.make_async_remote_copy(
                 own, held, i_send.at[i], i_recv.at[i], device_id=(kxs[d], ht, re), device_id_type=MESH
             ).start()
+    gather(ORDER[0])
     for c in ORDER[1:]:
         gather(c)
     local = [

time: 43 us -> 42.6 us (level)
  no operation moved by 1% of the time
where the time goes in v6:
time: 42.6 us; the launch traced here: 42.5 us
  Pallas kernels  41.8 us (98%)
  local copies, waits for them, and re-layouts  0.75 us (2%)
    pallas_call x1, Pallas kernels, local(): pl.pallas_call(kernel, out_shape=pltpu.VMEM(velocity.shape, F32), in_spec...  41.8 us

profile of v6, /device:TPU:1, one launch (start us, length us, event | category | flops | bytes accessed | tf_op | source)
XLA Modules:
  0.0 42.5 jit_solution(823001115372639723)
XLA Ops:
  0.0 41.8 %shard_map.73 = f32[3,1,4,64,128]{4,3,2,1,0:T(8,128)S(1)} custom-call(f32[3,1,4,64,128]{4,3,2,1,0:T(8,128)} %v.1, s32[8]{0:T(128)} %low_h.1, s32[4,8]{1,0:T(4,128)} %nb_own.1, s32[64]{0:T(128)} %omap_h.1, s32[4]{0:T(128)} %cnt_own.1, f32[1,512,512]{2,1,0:T(8,128)} %helm.1, bf16[3,128,256]{2,1,0:T(8,128)(2,1)} %constant.2.clone.table), custom_call_target="tpu_custom_call" | custom-call | tf_op jit(solution)/shard_map/pallas_call | solution.py:414
  41.8 0.7 %copy.9 = f32[3,1,4,64,128]{4,3,2,1,0:T(8,128)} copy(f32[3,1,4,64,128]{4,3,2,1,0:T(8,128)S(1)} %shard_map.73) | data formatting | bytes 786432
